TPU v7x, 32 devices: a whole 2x2x4 slice. The times are simulated.
32 devices in a mesh: ctx: 8 (over z, x), exp: 4 (over y, core).
Axes of the slice: x: 2, y: 2, z: 4, core: 2. Of those that a mesh axis runs over, the one named last changes fastest.
Arguments:
- attn_query: bfloat16 [8192, 2048], P('ctx', 'exp'), may hold values from -112 to 112
- attn_key: bfloat16 [8192, 2048], P('ctx', 'exp'), may hold values from -40 to 40
- attn_value: bfloat16 [8192, 2048], P('ctx', 'exp'), may hold values from -40 to 40
- prefix_state: float32 [8, 16, 128, 128], P('ctx', 'exp'), may hold values from -40960 to 40960
- moe_in: bfloat16 [8192, 2048], P(('ctx', 'exp')), may hold values from -6 to 6
- grad_out: bfloat16 [8192, 2048], P(('ctx', 'exp')), may hold values from -6 to 6
- router_gates: bfloat16 [8192, 1], P(('ctx', 'exp')), may hold values from 0.099609375 to 1
- expert_ids: int32 [8192, 1], P(('ctx', 'exp')), may hold values from 0 to 3; in each aligned block of 256 rows (0 to 255, 256 to 511, ...) at most 96 rows name the same one
- w_gate_up: bfloat16 [4, 2048, 1024], P('exp'), may hold values from -0.125 to 0.125
- w_down: bfloat16 [4, 512, 2048], P('exp'), may hold values from -0.25 to 0.25
- w_out: bfloat16 [2048, 2048], P('exp'), may hold values from -0.125 to 0.125
Outputs:
- grad_query: bfloat16 [8192, 2048], P('ctx', 'exp')
- grad_key: bfloat16 [8192, 2048], P('ctx', 'exp')
- grad_value: bfloat16 [8192, 2048], P('ctx', 'exp')
- grad_resid: bfloat16 [8192, 2048], P(('ctx', 'exp'))
- grad_gates: bfloat16 [8192, 1], P(('ctx', 'exp'))
- grad_gate_up: float32 [4, 2048, 1024], P('exp', 'ctx')
- grad_down: float32 [4, 512, 2048], P('exp', 'ctx')
Inputs may be any that keep to these rules, and one draw needn't show every extreme that they name: `expert_ids`: among the 256 rows of one device (aligned blocks of rows) no expert is named more than 96 times, a bound that some block reaches.
All inputs are finite; a program needn't handle non-finite values.
Results may differ from a plain program's by a relative error of at most 0.0063.
Values may be sent and summed in bfloat16 or wider, within the bound.
A program may use at most 192 MiB of HBM per device.

v0:
```python
import functools

import jax
import jax.numpy as jnp
from jax import lax
from jax.experimental import pallas as pl
from jax.experimental.pallas import tpu as pltpu
from jax.sharding import PartitionSpec as P

LANES = 128
MESH = pl.DeviceIdType.MESH
BF16 = jnp.bfloat16
F32 = jnp.float32


def contract_rows(left, right):
    return lax.dot_general(left, right, (((0,), (0,)), ((), ())), preferred_element_type=F32)


def contract_cols(left, right):
    return lax.dot_general(left, right, (((1,), (1,)), ((), ())), preferred_element_type=F32)


def plain(left, right):
    return jnp.dot(left, right, preferred_element_type=F32)


def bit_of(value, bit):
    return lax.rem(lax.div(value, bit), 2)


def flipped(value, mask):
    found, bit = value, 1
    while bit <= mask:
        if mask & bit:
            found = found + bit - 2 * bit * bit_of(value, bit)
        bit *= 2
    return found


def at_least(value, bound, size):
    return lax.div(value - bound + size, size)


class Sends:
    def __init__(self):
        self.open = []

    def start(self, src, dst, send, recv, device, when=None):
        copy = pltpu.make_async_remote_copy(
            src_ref=src, dst_ref=dst, send_sem=send, recv_sem=recv, device_id=device, device_id_type=MESH
        )
        self.open.append((copy, when))
        if when is None:
            copy.start()
        else:
            pl.when(when)(copy.start)
        return copy

    def drain(self):
        for copy, when in self.open:
            if when is None:
                copy.wait_send()
            else:
                pl.when(when)(copy.wait_send)


def layer_kernel(
    groups,
    blocks,
    chunk,
    target_ref,
    gates_ref,
    moe_ref,
    cot_ref,
    pair_hbm,
    back_hbm,
    proj_hbm,
    query_hbm,
    key_hbm,
    value_hbm,
    prior_hbm,
    dquery_ref,
    dkey_ref,
    dvalue_ref,
    resid_ref,
    dgates_ref,
    up_ref,
    down_ref,
    pair_ref,
    back_ref,
    proj_ref,
    query_ref,
    key_ref,
    value_ref,
    prior_ref,
    load_sem,
    targets_ref,
    target_sem,
    packed_ref,
    came_ref,
    token_sem,
    scaled_ref,
    both_ref,
    rows_t_ref,
    hidden_t_ref,
    gate_out_ref,
    gate_in_ref,
    gate_sem,
    rows_ref,
    rows_sem,
    slots_ref,
    grad_ref,
    scaled_grad_ref,
    local_ref,
    later_ref,
    line_ref,
    state_out_ref,
    state_in_ref,
    state_sem,
    pair_up_out,
    pair_up_in,
    pair_down_out,
    pair_down_in,
    pair_sem,
    line_up_out,
    line_up_in,
    line_down_out,
    line_down_in,
    line_sem,
):
    me, block = lax.axis_index("exp"), lax.axis_index("ctx")
    side, place = lax.rem(block, 2), lax.div(block, 2)
    length = blocks // 2
    tokens_own, width = moe_ref.shape
    capacity = came_ref.shape[1]
    hidden_units = back_ref.shape[0]
    heads, head_dim = prior_ref.shape[:2]
    tokens = query_ref.shape[0]
    sends = Sends()

    loads = []
    for at, (src, dst) in enumerate(
        [
            (pair_hbm, pair_ref),
            (back_hbm, back_ref),
            (proj_hbm, proj_ref),
            (query_hbm, query_ref),
            (key_hbm, key_ref),
            (value_hbm, value_ref),
            (prior_hbm, prior_ref),
        ]
    ):
        loads.append(pltpu.make_async_copy(src, dst, load_sem.at[at]))
        loads[-1].start()

    barrier = pltpu.get_barrier_semaphore()
    peers = [{"exp": flipped(me, k)} for k in range(1, groups)]
    shifts = [1]
    while shifts[-1] < blocks // 2:
        shifts.append(2 * shifts[-1])
    for shift in shifts:
        peers += [{"ctx": lax.rem(block + shift, blocks)}, {"ctx": lax.rem(block + blocks - shift, blocks)}]
    for peer in peers:
        pl.semaphore_signal(barrier, inc=1, device_id=peer, device_id_type=MESH)
    pl.semaphore_wait(barrier, len(peers))

    def near(k):
        return {"exp": flipped(me, k)}

    own_target = target_ref[0:1, :]

    def placing(expert, targets):
        spots = lax.broadcasted_iota(jnp.int32, (capacity, tokens_own), 0) + expert * capacity
        return jnp.where(spots == targets, 1.0, 0.0).astype(BF16)

    token_copies, target_copies = {}, {}
    for k in (2, 3, 1, 0):
        chosen = placing(flipped(me, k), own_target)
        out = packed_ref.at[k - 1] if k else came_ref.at[0]
        out[:, :width] = plain(chosen, moe_ref[...]).astype(BF16)
        out[:, width : 2 * width] = plain(chosen, cot_ref[...]).astype(BF16)
        out[:, 2 * width :] = plain(chosen, gates_ref[...]).astype(BF16)
        if k:
            token_copies[k] = sends.start(out, came_ref.at[k], token_sem.at[0, k], token_sem.at[1, k], near(k))
    targets_ref[0] = target_ref[...]
    for k in range(1, groups):
        target_copies[k] = sends.start(
            target_ref, targets_ref.at[k], target_sem.at[0, k], target_sem.at[1, k], near(k)
        )

    gate_copies, row_copies, relay_copies = {}, {}, {}

    def expert(which, part, begin, piece):
        for k in which:
            if k:
                token_copies[k].wait_recv()
        size = len(which) * capacity
        inner = pl.ds(begin, size)
        rows_in = jnp.concatenate([came_ref[k, :, :width] for k in which], axis=0)
        cot = jnp.concatenate([came_ref[k, :, width : 2 * width] for k in which], axis=0).astype(F32)
        gate = jnp.concatenate([came_ref[k, :, 2 * width :] for k in which], axis=0)[:, :1].astype(F32)
        scaled = (gate * cot).astype(BF16)
        scaled_ref[part, inner, :] = scaled
        both = plain(rows_in, pair_ref[...])
        first, second = both[:, :hidden_units], both[:, hidden_units:]
        logistic = jax.nn.sigmoid(first)
        silu = first * logistic
        hidden = (silu * second).astype(BF16)
        grad_hidden = contract_cols(scaled, back_ref[...])
        slope = logistic * (1.0 + first * (1.0 - logistic))
        both_ref[part, inner, :hidden_units] = (grad_hidden * second * slope).astype(BF16)
        both_ref[part, inner, hidden_units:] = (grad_hidden * silu).astype(BF16)
        grad_rows = contract_cols(both_ref[part, inner, :], pair_ref[...]).astype(BF16)
        at = pl.ds(part * 2 * capacity + begin, size)
        rows_ref[0, at, :] = (cot + grad_rows.astype(F32)).astype(BF16)
        for partner in (2, 1):
            row_copies[partner, piece] = sends.start(
                rows_ref.at[0, at], rows_ref.at[partner, at],
                rows_sem.at[0, partner, piece], rows_sem.at[1, partner, piece], near(partner),
            )
        output = plain(hidden, back_ref[...])
        grad_gate = jnp.sum(cot * output, axis=1, keepdims=True)
        for spot, k in enumerate(which):
            one = jnp.broadcast_to(grad_gate[spot * capacity : (spot + 1) * capacity], (capacity, LANES))
            if k:
                gate_out_ref[k - 1] = one.astype(BF16)
                gate_copies[k] = sends.start(
                    gate_out_ref.at[k - 1], gate_in_ref.at[k], gate_sem.at[0, k], gate_sem.at[1, k], near(k)
                )
            else:
                gate_in_ref[0] = one.astype(BF16)
        return hidden

    loads[0].wait()
    loads[1].wait()
    hidden = expert((0, 1), 0, 0, 0)
    hidden_t_ref[0] = hidden.T
    rows_t_ref[0] = jnp.concatenate([came_ref[0, :, :width], came_ref[1, :, :width]], axis=0).T
    hidden_2 = expert((2,), 1, 0, 1)
    hidden_3 = expert((3,), 1, capacity, 2)
    hidden_t_ref[1] = jnp.concatenate([hidden_2, hidden_3], axis=0).T
    rows_t_ref[1] = jnp.concatenate([came_ref[2, :, :width], came_ref[3, :, :width]], axis=0).T

    unit, unit_down = width // blocks, hidden_units // blocks

    def up_part(which):
        at = pl.ds(pl.multiple_of(which * unit, unit), unit)
        return plain(rows_t_ref[0, at, :], both_ref[0]) + plain(rows_t_ref[1, at, :], both_ref[1])

    def down_part(which):
        at = pl.ds(pl.multiple_of(which * unit_down, unit_down), unit_down)
        return plain(hidden_t_ref[0, at, :], scaled_ref[0]) + plain(hidden_t_ref[1, at, :], scaled_ref[1])

    right_half = lax.div(place, max(length // 2, 1))
    fewer = place * (1 - right_half) + (length - 1 - place) * right_half

    def item(j):
        both_ways = at_least(2 * fewer, j + 1, 4 * length)
        step = both_ways * (j // 2) + (1 - both_ways) * (j - fewer)
        major = 1 - both_ways * (j % 2)
        rightward = major * (1 - right_half) + (1 - major) * right_half
        return rightward * (length - 1 - step) + (1 - rightward) * step, rightward

    items = [item(j) for j in range(length - 1)] + [(place, None)]
    partner = {"ctx": block + 1 - 2 * side}
    pair_copies = []
    for j, (home, _) in enumerate(items):
        pair_up_out[j] = up_part(2 * home + 1 - side).astype(BF16)
        one = sends.start(pair_up_out.at[j], pair_up_in.at[j], pair_sem.at[0, 0, j], pair_sem.at[1, 0, j], partner)
        pair_down_out[j] = down_part(2 * home + 1 - side).astype(BF16)
        two = sends.start(pair_down_out.at[j], pair_down_in.at[j], pair_sem.at[0, 1, j], pair_sem.at[1, 1, j], partner)
        pair_copies.append((one, two))

    has_left, has_right = at_least(place, 1, 2 * length), at_least(length - 1 - place, 1, 2 * length)

    def came_along(kind, slot, buffer):
        pltpu.make_async_remote_copy(
            src_ref=buffer.at[slot], dst_ref=buffer.at[slot], send_sem=line_sem.at[0, kind, 0],
            recv_sem=line_sem.at[1, kind, slot], device_id=partner, device_id_type=MESH,
        ).wait_recv()

    def line_item(j):
        home, rightward = items[j]
        parts = [
            (0, up_ref, up_part, pair_up_in, line_up_out, line_up_in),
            (1, down_ref, down_part, pair_down_in, line_down_out, line_down_in),
        ]
        for kind, total, part, pair_in, out, line_in in parts:
            pair_copies[j][kind].wait_recv()
            total[...] = part(2 * home + side) + pair_in[j].astype(F32)
            if rightward is None:
                ways = [(has_left, place + 1), (has_right, place)]
            else:
                ways = [(rightward * has_left + (1 - rightward) * has_right, home + rightward)]
            for present, slot in ways:

                @pl.when(present == 1)
                def _():
                    came_along(kind, slot, line_in)
                    total[...] += line_in[slot].astype(F32)

            if rightward is not None:
                out[j] = total[...].astype(BF16)
                sends.start(
                    out.at[j], line_in.at[home + rightward], line_sem.at[0, kind, j],
                    line_sem.at[1, kind, home + rightward], {"ctx": block + 4 * rightward - 2},
                )

    pieces = [pl.ds(0, 2 * capacity), pl.ds(2 * capacity, capacity), pl.ds(3 * capacity, capacity)]
    loads[2].wait()

    def project(j, piece):
        slots_ref[j, pieces[piece], :] = contract_cols(rows_ref[j, pieces[piece], :], proj_ref[...]).astype(BF16)

    def relay(piece):
        row_copies[2, piece].wait_recv()
        relay_copies[piece] = sends.start(
            rows_ref.at[2, pieces[piece]], rows_ref.at[3, pieces[piece]],
            rows_sem.at[0, 3, piece], rows_sem.at[1, 3, piece], near(1),
        )

    for piece in range(3):
        project(0, piece)
    for piece in range(3):
        row_copies[1, piece].wait_recv()
        project(1, piece)
    relay(0)
    project(2, 0)
    relay_copies[0].wait_recv()
    project(3, 0)
    line_item(0)
    relay(1)
    project(2, 1)
    relay_copies[1].wait_recv()
    project(3, 1)
    relay(2)
    project(2, 2)
    relay_copies[2].wait_recv()
    project(3, 2)

    base = (3 * blocks + block) * tokens
    for at in (3, 4, 5):
        loads[at].wait()

    def inverse_counts(start, shape):
        counts = base + start + 1 + lax.broadcasted_iota(jnp.int32, shape, 0)
        return 1.0 / counts.astype(F32)

    for i in range(groups):
        if i:
            target_copies[i].wait_recv()
        targets = targets_ref[i, 0:1, :]
        chosen = jnp.concatenate([placing(flipped(me, j), targets) for j in range(groups)], axis=0)
        found = jnp.concatenate(
            [slots_ref[j, (j ^ i) * capacity : ((j ^ i) + 1) * capacity, :] for j in range(groups)], axis=0
        )
        start = pl.multiple_of(flipped(me, i) * tokens_own, tokens_own)
        at = pl.ds(start, tokens_own)
        grads = contract_rows(chosen, found)
        scaled = (grads * inverse_counts(start, grads.shape)).astype(BF16)
        grad_ref[at, :] = grads.astype(BF16)
        scaled_grad_ref[at, :] = scaled
        for h in range(heads):
            cols = slice(h * head_dim, (h + 1) * head_dim)
            state = contract_rows(query_ref[at, cols], scaled[:, cols])
            local_ref[h] = state + local_ref[h] if i else state

    state_out_ref[0] = local_ref[...].astype(BF16)
    pair_state = sends.start(state_out_ref.at[0], state_in_ref.at[0], state_sem.at[0, 0], state_sem.at[1, 0], partner)

    own = jnp.concatenate([placing(flipped(me, j), own_target) for j in range(groups)], axis=0)
    rows = jnp.concatenate([rows_ref[j, j * capacity : (j + 1) * capacity, :] for j in range(groups)], axis=0)
    resid_ref[...] = contract_rows(own, rows).astype(BF16)
    for k in range(1, groups):
        gate_copies[k].wait_recv()
    gates = jnp.concatenate([gate_in_ref[k] for k in range(groups)], axis=0)
    dgates_ref[...] = contract_rows(own, gates)[:, :1].astype(BF16)

    pair_state.wait_recv()
    local_ref[...] = local_ref[...] + state_in_ref[0].astype(F32)
    later_ref[...] = state_in_ref[0].astype(F32) * (1 - side).astype(F32)
    line_ref[...] = jnp.zeros_like(line_ref)
    turn, step, steps = 1, 1, []
    while step < length:
        steps.append((turn, step))
        turn, step = turn + 1, 2 * step

    def send_state(turn, step):
        state_out_ref[turn] = (local_ref[...] + line_ref[...]).astype(BF16)
        sends.start(
            state_out_ref.at[turn], state_in_ref.at[turn], state_sem.at[0, turn], state_sem.at[1, turn],
            {"ctx": lax.rem(block + blocks - 2 * step, blocks)}, when=place >= step,
        )

    def take_state(turn, step):
        @pl.when(place + step < length)
        def _():
            pltpu.make_async_remote_copy(
                src_ref=state_in_ref.at[turn], dst_ref=state_in_ref.at[turn], send_sem=state_sem.at[0, turn],
                recv_sem=state_sem.at[1, turn], device_id=partner, device_id_type=MESH,
            ).wait_recv()
            line_ref[...] += state_in_ref[turn].astype(F32)

    row = lax.broadcasted_iota(jnp.int32, (chunk, chunk), 0)
    col = lax.broadcasted_iota(jnp.int32, (chunk, chunk), 1)

    def forward(h, carry):
        cols = pl.ds(pl.multiple_of(h * head_dim, head_dim), head_dim)
        state = prior_ref[h]
        for at in range(tokens // chunk):
            rows = pl.ds(at * chunk, chunk)
            keys, values, grads = key_ref[rows, cols], value_ref[rows, cols], grad_ref[rows, cols]
            mix = jnp.where(col <= row, contract_cols(grads, values), 0.0).astype(BF16)
            out = plain(mix, keys) + contract_cols(grads, state.astype(BF16))
            dquery_ref[rows, cols] = (out * inverse_counts(at * chunk, out.shape)).astype(BF16)
            state = state + contract_rows(keys, values)
        return carry

    def backward(h, carry):
        cols = pl.ds(pl.multiple_of(h * head_dim, head_dim), head_dim)
        state = later_ref[h] + line_ref[h]
        for at in reversed(range(tokens // chunk)):
            rows = pl.ds(at * chunk, chunk)
            query, keys = query_ref[rows, cols], key_ref[rows, cols]
            values, scaled = value_ref[rows, cols], scaled_grad_ref[rows, cols]
            held = state.astype(BF16)
            mix_key = jnp.where(col >= row, contract_cols(values, scaled), 0.0).astype(BF16)
            dkey_ref[rows, cols] = (plain(mix_key, query) + contract_cols(values, held)).astype(BF16)
            mix_value = jnp.where(col >= row, contract_cols(keys, query), 0.0).astype(BF16)
            dvalue_ref[rows, cols] = (plain(mix_value, scaled) + plain(keys, held)).astype(BF16)
            state = state + contract_rows(query, scaled)
        return carry

    loads[6].wait()
    for at, (turn, step) in enumerate(steps):
        send_state(turn, step)
        if at == 0:
            if length > 2:
                line_item(1)
            lax.fori_loop(0, heads, forward, 0)
        take_state(turn, step)
    lax.fori_loop(0, heads, backward, 0)
    for j in range(2, length):
        line_item(j)
    sends.drain()


def compute(
    attn_query, attn_key, attn_value, prefix_state, moe_in, grad_out, router_gates, expert_ids,
    w_gate_up, w_down, w_out,
):
    groups, blocks = lax.axis_size("exp"), lax.axis_size("ctx")
    rows, width = moe_in.shape
    capacity = 3 * rows // (2 * groups * w_gate_up.shape[0])
    flat_ids = expert_ids.reshape(rows)
    place = jnp.arange(rows, dtype=jnp.int32)
    same = (flat_ids[:, None] == flat_ids[None, :]) & (place[:, None] < place[None, :])
    target = flat_ids * capacity + jnp.sum(same.astype(jnp.int32), axis=0)
    target = jnp.broadcast_to(target[None, :], (8, rows))
    gates = jnp.broadcast_to(router_gates, (rows, LANES))
    hidden_units, wide = w_down.shape[1], w_gate_up.shape[2]
    unit, unit_down = width // blocks, hidden_units // blocks
    tokens, cols = attn_query.shape
    heads, head_dim = prefix_state.shape[1:3]
    length = blocks // 2
    turns = max(length.bit_length(), 1)
    whole = pl.BlockSpec(memory_space=pltpu.VMEM)
    away = pl.BlockSpec(memory_space=pl.ANY)
    flat = jax.ShapeDtypeStruct((tokens, cols), BF16)
    dma = pltpu.SemaphoreType.DMA
    vmem = pltpu.VMEM
    scratch = [
        vmem((width, wide), BF16), vmem((hidden_units, width), BF16), vmem((cols, width), BF16),
        vmem((tokens, cols), BF16), vmem((tokens, cols), BF16), vmem((tokens, cols), BF16),
        vmem((heads, head_dim, head_dim), F32), dma((7,)),
        vmem((groups, 8, rows), jnp.int32), dma((2, groups)),
        vmem((groups - 1, capacity, 2 * width + LANES), BF16),
        vmem((groups, capacity, 2 * width + LANES), BF16), dma((2, groups)),
        vmem((2, 2 * capacity, width), BF16), vmem((2, 2 * capacity, wide), BF16),
        vmem((2, width, 2 * capacity), BF16), vmem((2, hidden_units, 2 * capacity), BF16),
        vmem((groups - 1, capacity, LANES), BF16), vmem((groups, capacity, LANES), BF16), dma((2, groups)),
        vmem((groups, groups * capacity, width), BF16), dma((2, groups, 3)),
        vmem((groups, groups * capacity, cols), BF16),
        vmem((tokens, cols), BF16), vmem((tokens, cols), BF16),
        vmem((heads, head_dim, head_dim), F32), vmem((heads, head_dim, head_dim), F32),
        vmem((heads, head_dim, head_dim), F32),
        vmem((turns, heads, head_dim, head_dim), BF16), vmem((turns, heads, head_dim, head_dim), BF16),
        dma((2, turns)),
        vmem((length, unit, wide), BF16), vmem((length, unit, wide), BF16),
        vmem((length, unit_down, width), BF16), vmem((length, unit_down, width), BF16), dma((2, 2, length)),
        vmem((length - 1, unit, wide), BF16), vmem((length + 1, unit, wide), BF16),
        vmem((length - 1, unit_down, width), BF16), vmem((length + 1, unit_down, width), BF16),
        dma((2, 2, length + 1)),
    ]
    return pl.pallas_call(
        functools.partial(layer_kernel, groups, blocks, min(256, tokens)),
        in_specs=[whole] * 4 + [away] * 7,
        out_specs=[whole] * 7,
        out_shape=[
            flat, flat, flat, jax.ShapeDtypeStruct((rows, width), BF16), jax.ShapeDtypeStruct((rows, 1), BF16),
            jax.ShapeDtypeStruct((unit, wide), F32), jax.ShapeDtypeStruct((unit_down, width), F32),
        ],
        scratch_shapes=scratch,
        compiler_params=pltpu.CompilerParams(
            collective_id=0, has_side_effects=True, vmem_limit_bytes=67043328
        ),
        name="layer",
    )(
        target, gates, moe_in, grad_out, w_gate_up[0], w_down[0], w_out, attn_query, attn_key, attn_value,
        prefix_state[0],
    )


def on_device(*args):
    dquery, dkey, dvalue, resid, dgates, up, down = compute(*args)
    return dquery, dkey, dvalue, resid, dgates, up[None], down[None]


def solution(mesh):
    return jax.shard_map(
        on_device,
        mesh=mesh,
        in_specs=(
            P("ctx", "exp"),
            P("ctx", "exp"),
            P("ctx", "exp"),
            P("ctx", "exp", None, None),
            P(("ctx", "exp"), None),
            P(("ctx", "exp"), None),
            P(("ctx", "exp"), None),
            P(("ctx", "exp"), None),
            P("exp", None, None),
            P("exp", None, None),
            P("exp", None),
        ),
        out_specs=(
            P("ctx", "exp"),
            P("ctx", "exp"),
            P("ctx", "exp"),
            P(("ctx", "exp"), None),
            P(("ctx", "exp"), None),
            P("exp", "ctx", None),
            P("exp", "ctx", None),
        ),
        check_vma=False,
    )
```

profile of v0, /device:TPU:16, one launch (start us, length us, event | category | flops | bytes accessed | tf_op | source)
XLA Modules:
  0.0 182.2 jit_solution(16478657860387789100)
XLA Ops:
  0.6 0.7 reduce
  1.3 0.9 convert_reduce_fusion
  2.2 0.7 multiply_add_fusion
  2.9 0.6 broadcast_in_dim.10.target_ref
  3.5 0.7 broadcast_in_dim.23.gates_ref
  4.2 169.3 %layer.1 = (bf16[1024,512]{1,0:T(8,128)(2,1)}, bf16[1024,512]{1,0:T(8,128)(2,1)}, bf16[1024,512]{1,0:T(8,128)(2,1)}, bf16[256,2048]{1,0:T(8,128)(2,1)}, bf16[256...) custom-call(s32[8,256]{1,0:T(8,128)} %broadcast_in_dim.10.target_ref, ...), custom_call_target="tpu_custom_call" | custom-call | tf_op jit(solution)/shard_map/layer/pallas_call | solution.py:496
  173.5 0.0 copy-start.3
  173.5 1.6 copy.19
  175.1 0.0 copy-start.2
  175.1 2.4 %copy.26 = bf16[1024,512]{1,0:T(8,128)(2,1)} copy(bf16[1024,512]{1,0:T(8,128)(2,1)} %get-tuple-element.42) | data formatting | bytes 2097152
  177.5 0.0 copy-done.3
  177.5 0.0 copy-start.1
  177.5 1.0 copy.27
  178.4 0.0 copy-done.2
  178.4 0.0 copy-start
  178.4 1.0 copy.28
  179.4 0.0 copy-done.1
  179.4 0.0 copy-start.4
  179.4 1.0 copy.29
  180.4 0.0 copy-done
  180.4 1.0 copy.30
  181.4 0.0 copy-done.4
  181.4 0.8 copy.31
Async XLA Ops:
  173.5 3.9 %copy-start.3 = (bf16[1024,512]{1,0:T(8,128)(2,1)S(1)}, bf16[1024,512]{1,0:T(8,128)(2,1)}, u32[]{:S(2)}) copy-start(bf16[1024,512]{1,0:T(8,128)(2,1)} %get-tuple-element.43) | copy-start | bytes 3145732
  175.1 3.3 %copy-start.2 = (bf16[1024,512]{1,0:T(8,128)(2,1)S(1)}, bf16[1024,512]{1,0:T(8,128)(2,1)}, u32[]{:S(2)}) copy-start(bf16[1024,512]{1,0:T(8,128)(2,1)} %get-tuple-element.44) | copy-start | bytes 3145732
  177.5 1.9 %copy-start.1 = (bf16[256,2048]{1,0:T(8,128)(2,1)S(1)}, bf16[256,2048]{1,0:T(8,128)(2,1)}, u32[]{:S(2)}) copy-start(bf16[256,2048]{1,0:T(8,128)(2,1)} %get-tuple-element.45) | copy-start | bytes 3145732
  178.4 1.9 %copy-start = (f32[256,1024]{1,0:T(8,128)S(1)}, f32[256,1024]{1,0:T(8,128)}, u32[]{:S(2)}) copy-start(f32[256,1024]{1,0:T(8,128)} %get-tuple-element.19) | copy-start | bytes 3145732
  179.4 1.9 %copy-start.4 = (f32[64,2048]{1,0:T(8,128)S(1)}, f32[64,2048]{1,0:T(8,128)}, u32[]{:S(2)}) copy-start(f32[64,2048]{1,0:T(8,128)} %get-tuple-element.20) | copy-start | bytes 1572868
where the time goes:
time: 182 us
  Pallas kernels  169 us (93%)
  local copies, waits for them, and re-layouts  9.95 us (5%)
  other arithmetic  2.25 us (1%)
    pallas_call x1, Pallas kernels, compute(): pl.pallas_call(functools.partial(layer_kernel, groups, blocks, min(256, t...  169 us
    unnamed x17, local copies, waits for them, and re-layouts  8.62 us

commit v1 on v0

v1 whole, which is shorter than its diff:
```python
import functools

import jax
import jax.numpy as jnp
from jax import lax
from jax.experimental import pallas as pl
from jax.experimental.pallas import tpu as pltpu
from jax.sharding import PartitionSpec as P

LANES = 128
MESH = pl.DeviceIdType.MESH
BF16 = jnp.bfloat16
F32 = jnp.float32


def contract_rows(left, right):
    return lax.dot_general(left, right, (((0,), (0,)), ((), ())), preferred_element_type=F32)


def contract_cols(left, right):
    return lax.dot_general(left, right, (((1,), (1,)), ((), ())), preferred_element_type=F32)


def plain(left, right):
    return jnp.dot(left, right, preferred_element_type=F32)


def bit_of(value, bit):
    return lax.rem(lax.div(value, bit), 2)


def flipped(value, mask):
    found, bit = value, 1
    while bit <= mask:
        if mask & bit:
            found = found + bit - 2 * bit * bit_of(value, bit)
        bit *= 2
    return found


def at_least(value, bound, size):
    return lax.div(value - bound + size, size)


class Sends:
    def __init__(self):
        self.open = []

    def start(self, src, dst, send, recv, device, when=None):
        copy = pltpu.make_async_remote_copy(
            src_ref=src, dst_ref=dst, send_sem=send, recv_sem=recv, device_id=device, device_id_type=MESH
        )
        self.open.append((copy, when))
        if when is None:
            copy.start()
        else:
            pl.when(when)(copy.start)
        return copy

    def drain(self):
        for copy, when in self.open:
            if when is None:
                copy.wait_send()
            else:
                pl.when(when)(copy.wait_send)


def layer_kernel(groups, blocks, chunk, direct, *refs):
    (
        ids_ref, gates_ref, moe_ref, cot_ref, pair_hbm, back_hbm, proj_hbm, query_hbm, key_hbm, value_hbm, prior_hbm,
        dquery_hbm, dkey_hbm, dvalue_hbm, resid_hbm, dgates_ref, up_hbm, down_hbm,
        pair_ref, back_ref, proj_ref, query_ref, key_ref, value_ref, prior_ref, load_sem,
        dquery_ref, dkey_ref, dvalue_ref, resid_ref, up_ref, down_ref, store_sem,
        targets_ref, target_sem, packed_ref, came_ref, token_sem,
        scaled_ref, both_ref, hidden_t_ref, gate_out_ref, gate_in_ref, gate_sem,
        rows_ref, rows_sem, slots_ref, grad_ref, scaled_grad_ref,
        local_ref, later_ref, line_ref, state_out_ref, state_in_ref, state_sem,
        pair_down_out, pair_down_in, pair_sem,
        line_up_out, line_up_in, line_down_out, line_down_in, line_sem,
    ) = refs[:63]
    if direct:
        other_rows_ref, other_both_ref, other_sem = refs[63:]
    else:
        rows_t_ref, pair_up_out, pair_up_in = refs[63:]
    me, block = lax.axis_index("exp"), lax.axis_index("ctx")
    side, place = lax.rem(block, 2), lax.div(block, 2)
    length = blocks // 2
    tokens_own, width = moe_ref.shape
    capacity = came_ref.shape[1]
    hidden_units = back_ref.shape[0]
    heads, head_dim = prior_ref.shape[:2]
    tokens = query_ref.shape[0]
    unit, unit_down = width // blocks, hidden_units // blocks
    partner = {"ctx": block + 1 - 2 * side}
    sends = Sends()

    loads = []
    for at, (src, dst) in enumerate(
        [
            (pair_hbm, pair_ref), (back_hbm, back_ref), (proj_hbm, proj_ref), (query_hbm, query_ref),
            (key_hbm, key_ref), (value_hbm, value_ref), (prior_hbm, prior_ref),
        ]
    ):
        loads.append(pltpu.make_async_copy(src, dst, load_sem.at[at]))
        loads[-1].start()
    stores = []

    def store(src, dst):
        stores.append(pltpu.make_async_copy(src, dst, store_sem.at[len(stores)]))
        stores[-1].start()

    barrier = pltpu.get_barrier_semaphore()
    peers = [{"exp": flipped(me, k)} for k in range(1, groups)]
    shifts = [1]
    while shifts[-1] < blocks // 2:
        shifts.append(2 * shifts[-1])
    for shift in shifts:
        peers += [{"ctx": lax.rem(block + shift, blocks)}, {"ctx": lax.rem(block + blocks - shift, blocks)}]
    for peer in peers:
        pl.semaphore_signal(barrier, inc=1, device_id=peer, device_id_type=MESH)

    def near(k):
        return {"exp": flipped(me, k)}

    ids = ids_ref[...]
    experts = lax.broadcasted_iota(jnp.int32, (8, tokens_own), 0)
    member = jnp.where(experts == ids, 1.0, 0.0)
    earlier = jnp.where(
        lax.broadcasted_iota(jnp.int32, (tokens_own, tokens_own), 0)
        < lax.broadcasted_iota(jnp.int32, (tokens_own, tokens_own), 1), 1.0, 0.0,
    )
    slot = jnp.sum(plain(member.astype(BF16), earlier.astype(BF16)) * member, axis=0, keepdims=True)
    own_target = ids * capacity + slot.astype(jnp.int32)
    targets_ref[0] = jnp.broadcast_to(own_target, (8, tokens_own))
    gates_row = gates_ref[...].astype(F32)

    def placing(expert, targets):
        spots = lax.broadcasted_iota(jnp.int32, (capacity, tokens_own), 0) + expert * capacity
        return jnp.where(spots == targets, 1.0, 0.0)

    token_copies, target_copies = {}, {}
    for k in (2, 3, 1, 0):
        found = placing(flipped(me, k), own_target)
        chosen = found.astype(BF16)
        out = packed_ref.at[k - 1] if k else came_ref.at[0]
        out[:, :width] = plain(chosen, moe_ref[...]).astype(BF16)
        out[:, width : 2 * width] = plain(chosen, cot_ref[...]).astype(BF16)
        gate = jnp.sum(found * gates_row, axis=1, keepdims=True)
        out[:, 2 * width :] = jnp.broadcast_to(gate, (capacity, LANES)).astype(BF16)
        if k == 2:
            pl.semaphore_wait(barrier, len(peers))
        if k:
            token_copies[k] = [
                sends.start(
                    out.at[:, cols], came_ref.at[k, :, cols], token_sem.at[0, k, half], token_sem.at[1, k, half], near(k)
                )
                for half, cols in enumerate((pl.ds(0, width), pl.ds(width, width + LANES)))
            ]
    for k in range(1, groups):
        target_copies[k] = sends.start(
            targets_ref.at[0], targets_ref.at[k], target_sem.at[0, k], target_sem.at[1, k], near(k)
        )

    gate_copies, row_copies, relay_copies = {}, {}, {}
    other_copies = []

    def other(src, dst):
        at = len(other_copies)
        other_copies.append(sends.start(src, dst, other_sem.at[0, at], other_sem.at[1, at], partner))

    def expert(which, part, begin, piece):
        size = len(which) * capacity
        inner = pl.ds(begin, size)
        for spot, k in enumerate(which):
            if k:
                token_copies[k][0].wait_recv()
            if direct:
                for home in range(length):
                    cols = pl.ds(pl.multiple_of((2 * home + 1 - side) * unit, unit), unit)
                    spots = pl.ds(begin + spot * capacity, capacity)
                    other(came_ref.at[k, :, cols], other_rows_ref.at[part, spots, pl.ds(home * unit, unit)])
        rows_in = jnp.concatenate([came_ref[k, :, :width] for k in which], axis=0)
        both = plain(rows_in, pair_ref[...])
        first, second = both[:, :hidden_units], both[:, hidden_units:]
        logistic = jax.nn.sigmoid(first)
        silu = first * logistic
        hidden = (silu * second).astype(BF16)
        slope = logistic * (1.0 + first * (1.0 - logistic))
        for k in which:
            if k:
                token_copies[k][1].wait_recv()
        cot = jnp.concatenate([came_ref[k, :, width : 2 * width] for k in which], axis=0).astype(F32)
        gate = jnp.concatenate([came_ref[k, :, 2 * width :] for k in which], axis=0)[:, :1].astype(F32)
        scaled = (gate * cot).astype(BF16)
        scaled_ref[part, inner, :] = scaled
        grad_hidden = contract_cols(scaled, back_ref[...])
        both_ref[part, inner, :hidden_units] = (grad_hidden * second * slope).astype(BF16)
        both_ref[part, inner, hidden_units:] = (grad_hidden * silu).astype(BF16)
        if direct:
            other(both_ref.at[part, inner], other_both_ref.at[part, inner])
        grad_rows = contract_cols(both_ref[part, inner, :], pair_ref[...]).astype(BF16)
        at = pl.ds(part * 2 * capacity + begin, size)
        rows_ref[0, at, :] = (cot + grad_rows.astype(F32)).astype(BF16)
        for peer in (2, 1):
            row_copies[peer, piece] = sends.start(
                rows_ref.at[0, at], rows_ref.at[peer, at],
                rows_sem.at[0, peer, piece], rows_sem.at[1, peer, piece], near(peer),
            )
        output = plain(hidden, back_ref[...])
        grad_gate = jnp.sum(cot * output, axis=1, keepdims=True)
        for spot, k in enumerate(which):
            one = jnp.broadcast_to(grad_gate[spot * capacity : (spot + 1) * capacity], (capacity, LANES))
            if k:
                gate_out_ref[k - 1] = one.astype(BF16)
                gate_copies[k] = sends.start(
                    gate_out_ref.at[k - 1], gate_in_ref.at[k], gate_sem.at[0, k], gate_sem.at[1, k], near(k)
                )
            else:
                gate_in_ref[0] = one.astype(BF16)
        return hidden

    pieces = [pl.ds(0, 2 * capacity), pl.ds(2 * capacity, capacity), pl.ds(3 * capacity, capacity)]

    def project(j, piece):
        slots_ref[j, pieces[piece], :] = contract_cols(rows_ref[j, pieces[piece], :], proj_ref[...]).astype(BF16)

    def project_near(piece):
        project(0, piece)
        row_copies[1, piece].wait_recv()
        project(1, piece)

    def project_far(piece):
        row_copies[2, piece].wait_recv()
        relay_copies[piece] = sends.start(
            rows_ref.at[2, pieces[piece]], rows_ref.at[3, pieces[piece]],
            rows_sem.at[0, 3, piece], rows_sem.at[1, 3, piece], near(1),
        )
        project(2, piece)
        relay_copies[piece].wait_recv()
        project(3, piece)

    loads[0].wait()
    loads[1].wait()
    hidden_t_ref[0] = expert((0, 1), 0, 0, 0).T
    if not direct:
        rows_t_ref[0] = jnp.concatenate([came_ref[0, :, :width], came_ref[1, :, :width]], axis=0).T
    loads[2].wait()
    project_near(0)
    hidden_2 = expert((2,), 1, 0, 1)
    project_near(1)
    hidden_3 = expert((3,), 1, capacity, 2)
    hidden_t_ref[1] = jnp.concatenate([hidden_2, hidden_3], axis=0).T
    if not direct:
        rows_t_ref[1] = jnp.concatenate([came_ref[2, :, :width], came_ref[3, :, :width]], axis=0).T

    def up_rows(which):
        at = pl.ds(pl.multiple_of(which * unit, unit), unit)
        return plain(rows_t_ref[0, at, :], both_ref[0]) + plain(rows_t_ref[1, at, :], both_ref[1])

    def up_pair(j, home):
        if not direct:
            pair_copies[0, j].wait_recv()
            return up_rows(2 * home + side) + pair_up_in[j].astype(F32)
        cols = pl.ds(pl.multiple_of((2 * home + side) * unit, unit), unit)
        there = pl.ds(pl.multiple_of(home * unit, unit), unit)
        found = None
        for part in range(2):
            here = jnp.concatenate([came_ref[2 * part, :, cols], came_ref[2 * part + 1, :, cols]], axis=0)
            one = contract_rows(here, both_ref[part])
            one = one + contract_rows(other_rows_ref[part, :, there], other_both_ref[part])
            found = one if found is None else found + one
        return found

    def down_rows(which):
        at = pl.ds(pl.multiple_of(which * unit_down, unit_down), unit_down)
        return plain(hidden_t_ref[0, at, :], scaled_ref[0]) + plain(hidden_t_ref[1, at, :], scaled_ref[1])

    right_half = lax.div(place, max(length // 2, 1))
    fewer = place * (1 - right_half) + (length - 1 - place) * right_half

    def item(j):
        both_ways = at_least(2 * fewer, j + 1, 4 * length)
        step = both_ways * (j // 2) + (1 - both_ways) * (j - fewer)
        major = 1 - both_ways * (j % 2)
        rightward = major * (1 - right_half) + (1 - major) * right_half
        return rightward * (length - 1 - step) + (1 - rightward) * step, rightward

    items = [item(j) for j in range(length - 1)] + [(place, None)]
    pair_copies = {}

    def pair_sends():
        for j, (home, _) in enumerate(items):
            if not direct:
                pair_up_out[j] = up_rows(2 * home + 1 - side).astype(BF16)
                pair_copies[0, j] = sends.start(
                    pair_up_out.at[j], pair_up_in.at[j], pair_sem.at[0, 0, j], pair_sem.at[1, 0, j], partner
                )
            pair_down_out[j] = down_rows(2 * home + 1 - side).astype(BF16)
            pair_copies[1, j] = sends.start(
                pair_down_out.at[j], pair_down_in.at[j], pair_sem.at[0, 1, j], pair_sem.at[1, 1, j], partner
            )

    has_left, has_right = at_least(place, 1, 2 * length), at_least(length - 1 - place, 1, 2 * length)
    inside = has_left * has_right

    def line_copy(kind, j, slot, device):
        out, line_in = ((line_up_out, line_up_in), (line_down_out, line_down_in))[kind]
        return pltpu.make_async_remote_copy(
            src_ref=out.at[j], dst_ref=line_in.at[slot], send_sem=line_sem.at[0, kind, j],
            recv_sem=line_sem.at[1, kind, slot], device_id=device, device_id_type=MESH,
        )

    def line_item(kind, j):
        home, rightward = items[j]
        total, out, line_in = ((up_ref, line_up_out, line_up_in), (down_ref, line_down_out, line_down_in))[kind]
        if kind:
            pair_copies[1, j].wait_recv()
            total[...] = down_rows(2 * home + side) + pair_down_in[j].astype(F32)
        else:
            total[...] = up_pair(j, home)
        if rightward is None:
            ways = [(has_left, place + 1), (has_right, place)]
        else:
            ways = [(rightward * has_left + (1 - rightward) * has_right, home + rightward)]
        for present, slot in ways:

            @pl.when(present == 1)
            def _():
                line_copy(kind, 0, slot, partner).wait_recv()
                total[...] += line_in[slot].astype(F32)

        if rightward is not None:
            out[j] = total[...].astype(BF16)
            line_copy(kind, j, home + rightward, {"ctx": block + 4 * rightward - 2}).start()

    def ends(*which):
        @pl.when(inside == 0)
        def _():
            for kind, j in which:
                if j < length - 1:
                    line_item(kind, j)

    def middles(*which):
        @pl.when(inside == 1)
        def _():
            for kind, j in which:
                if j < length - 1:
                    line_item(kind, j)

    pair_sends()
    project_near(2)
    for copy in other_copies:
        copy.wait_recv()
    ends((0, 0), (0, 1))
    project_far(0)
    middles((0, 0))
    project_far(1)
    ends((1, 0))
    project_far(2)

    base = (3 * blocks + block) * tokens
    for at in (3, 4, 5):
        loads[at].wait()

    def inverse_counts(start, shape):
        counts = base + start + 1 + lax.broadcasted_iota(jnp.int32, shape, 0)
        return 1.0 / counts.astype(F32)

    for i in range(groups):
        if i:
            target_copies[i].wait_recv()
        targets = targets_ref[i, 0:1, :]
        chosen = jnp.concatenate([placing(flipped(me, j), targets).astype(BF16) for j in range(groups)], axis=0)
        found = jnp.concatenate(
            [slots_ref[j, (j ^ i) * capacity : ((j ^ i) + 1) * capacity, :] for j in range(groups)], axis=0
        )
        start = pl.multiple_of(flipped(me, i) * tokens_own, tokens_own)
        at = pl.ds(start, tokens_own)
        grads = contract_rows(chosen, found)
        scaled = (grads * inverse_counts(start, grads.shape)).astype(BF16)
        grad_ref[at, :] = grads.astype(BF16)
        scaled_grad_ref[at, :] = scaled
        for h in range(heads):
            cols = slice(h * head_dim, (h + 1) * head_dim)
            state = contract_rows(query_ref[at, cols], scaled[:, cols])
            local_ref[h] = state + local_ref[h] if i else state

    state_out_ref[0] = local_ref[...].astype(BF16)
    pair_state = sends.start(state_out_ref.at[0], state_in_ref.at[0], state_sem.at[0, 0], state_sem.at[1, 0], partner)
    middles((0, 1))

    own = jnp.concatenate([placing(flipped(me, j), own_target).astype(BF16) for j in range(groups)], axis=0)
    rows = jnp.concatenate([rows_ref[j, j * capacity : (j + 1) * capacity, :] for j in range(groups)], axis=0)
    resid_ref[...] = contract_rows(own, rows).astype(BF16)
    store(resid_ref, resid_hbm)
    for k in range(1, groups):
        gate_copies[k].wait_recv()
    gates = jnp.concatenate([gate_in_ref[k] for k in range(groups)], axis=0)
    dgates_ref[...] = contract_rows(gates, own)[0:1, :].astype(BF16)

    pair_state.wait_recv()
    local_ref[...] = local_ref[...] + state_in_ref[0].astype(F32)
    later_ref[...] = state_in_ref[0].astype(F32) * (1 - side).astype(F32)
    line_ref[...] = jnp.zeros_like(line_ref)
    turn, step, steps = 1, 1, []
    while step < length:
        steps.append((turn, step))
        turn, step = turn + 1, 2 * step

    def send_state(turn, step):
        state_out_ref[turn] = (local_ref[...] + line_ref[...]).astype(BF16)
        sends.start(
            state_out_ref.at[turn], state_in_ref.at[turn], state_sem.at[0, turn], state_sem.at[1, turn],
            {"ctx": lax.rem(block + blocks - 2 * step, blocks)}, when=place >= step,
        )

    def take_state(turn, step):
        @pl.when(place + step < length)
        def _():
            pltpu.make_async_remote_copy(
                src_ref=state_in_ref.at[turn], dst_ref=state_in_ref.at[turn], send_sem=state_sem.at[0, turn],
                recv_sem=state_sem.at[1, turn], device_id=partner, device_id_type=MESH,
            ).wait_recv()
            line_ref[...] += state_in_ref[turn].astype(F32)

    row = lax.broadcasted_iota(jnp.int32, (chunk, chunk), 0)
    col = lax.broadcasted_iota(jnp.int32, (chunk, chunk), 1)

    def forward(h, carry):
        cols = pl.ds(pl.multiple_of(h * head_dim, head_dim), head_dim)
        state = prior_ref[h]
        for at in range(tokens // chunk):
            rows = pl.ds(at * chunk, chunk)
            keys, values, grads = key_ref[rows, cols], value_ref[rows, cols], grad_ref[rows, cols]
            mix = jnp.where(col <= row, contract_cols(grads, values), 0.0).astype(BF16)
            out = plain(mix, keys) + contract_cols(grads, state.astype(BF16))
            dquery_ref[rows, cols] = (out * inverse_counts(at * chunk, out.shape)).astype(BF16)
            state = state + contract_rows(keys, values)
        return carry

    def backward(h, carry):
        cols = pl.ds(pl.multiple_of(h * head_dim, head_dim), head_dim)
        state = later_ref[h] + line_ref[h]
        for at in reversed(range(tokens // chunk)):
            rows = pl.ds(at * chunk, chunk)
            query, keys = query_ref[rows, cols], key_ref[rows, cols]
            values, scaled = value_ref[rows, cols], scaled_grad_ref[rows, cols]
            held = state.astype(BF16)
            mix_key = jnp.where(col >= row, contract_cols(values, scaled), 0.0).astype(BF16)
            dkey_ref[rows, cols] = (plain(mix_key, query) + contract_cols(values, held)).astype(BF16)
            mix_value = jnp.where(col >= row, contract_cols(keys, query), 0.0).astype(BF16)
            dvalue_ref[rows, cols] = (plain(mix_value, scaled) + plain(keys, held)).astype(BF16)
            state = state + contract_rows(query, scaled)
        return carry

    loads[6].wait()
    if steps:
        send_state(*steps[0])
    for j in range(2, length - 1):
        line_item(0, j)
    lax.fori_loop(0, heads, forward, 0)
    store(dquery_ref, dquery_hbm)
    for at, one in enumerate(steps):
        if at:
            send_state(*one)
            if at == 1:
                middles((1, 0))
                for j in range(1, length - 1):
                    line_item(1, j)
        take_state(*one)
    lax.fori_loop(0, heads, backward, 0)
    store(dkey_ref, dkey_hbm)
    store(dvalue_ref, dvalue_hbm)
    line_item(0, length - 1)
    store(up_ref, up_hbm)
    line_item(1, length - 1)
    store(down_ref, down_hbm)
    for copy in stores:
        copy.wait()
    for kind in range(2):
        for j in range(length - 1):
            line_copy(kind, j, 0, partner).wait_send()
    sends.drain()


def pass_kernel(*refs):
    half = len(refs) // 2
    for src, dst in zip(refs[:half], refs[half:]):
        dst[...] = src[...]


def pass_on(*arrays):
    steps = 4
    specs = [
        pl.BlockSpec(one.shape, lambda i: (0, 0))
        if one.shape[0] % (16 * steps)
        else pl.BlockSpec((one.shape[0] // steps, one.shape[1]), lambda i: (i, 0))
        for one in arrays
    ]
    return pl.pallas_call(
        pass_kernel,
        grid=(steps,),
        in_specs=specs,
        out_specs=specs,
        out_shape=[jax.ShapeDtypeStruct(one.shape, one.dtype) for one in arrays],
        name="pass_on",
    )(*arrays)


def compute(
    attn_query, attn_key, attn_value, prefix_state, moe_in, grad_out, router_gates, expert_ids,
    w_gate_up, w_down, w_out,
):
    groups, blocks = lax.axis_size("exp"), lax.axis_size("ctx")
    rows, width = moe_in.shape
    capacity = 3 * rows // (2 * groups * w_gate_up.shape[0])
    hidden_units, wide = w_down.shape[1], w_gate_up.shape[2]
    unit, unit_down = width // blocks, hidden_units // blocks
    tokens, cols = attn_query.shape
    heads, head_dim = prefix_state.shape[1:3]
    length = blocks // 2
    turns = max(length.bit_length(), 1)
    direct = unit % LANES == 0
    whole = pl.BlockSpec(memory_space=pltpu.VMEM)
    away = pl.BlockSpec(memory_space=pl.ANY)
    flat = jax.ShapeDtypeStruct((tokens, cols), BF16)
    dma = pltpu.SemaphoreType.DMA
    vmem = pltpu.VMEM
    state = vmem((heads, head_dim, head_dim), F32)
    flat_ref = vmem((tokens, cols), BF16)
    scratch = [
        vmem((width, wide), BF16), vmem((hidden_units, width), BF16), vmem((cols, width), BF16),
        flat_ref, flat_ref, flat_ref, state, dma((7,)),
        flat_ref, flat_ref, flat_ref, vmem((rows, width), BF16), vmem((unit, wide), F32),
        vmem((unit_down, width), F32), dma((6,)),
        vmem((groups, 8, rows), jnp.int32), dma((2, groups)),
        vmem((groups - 1, capacity, 2 * width + LANES), BF16),
        vmem((groups, capacity, 2 * width + LANES), BF16), dma((2, groups, 2)),
        vmem((2, 2 * capacity, width), BF16), vmem((2, 2 * capacity, wide), BF16),
        vmem((2, hidden_units, 2 * capacity), BF16),
        vmem((groups - 1, capacity, LANES), BF16), vmem((groups, capacity, LANES), BF16), dma((2, groups)),
        vmem((groups, groups * capacity, width), BF16), dma((2, groups, 3)),
        vmem((groups, groups * capacity, cols), BF16),
        flat_ref, flat_ref,
        state, state, state,
        vmem((turns, heads, head_dim, head_dim), BF16), vmem((turns, heads, head_dim, head_dim), BF16),
        dma((2, turns)),
        vmem((length, unit_down, width), BF16), vmem((length, unit_down, width), BF16), dma((2, 2, length)),
        vmem((length - 1, unit, wide), BF16), vmem((length + 1, unit, wide), BF16),
        vmem((length - 1, unit_down, width), BF16), vmem((length + 1, unit_down, width), BF16),
        dma((2, 2, length + 1)),
    ]
    if direct:
        scratch += [
            vmem((2, 2 * capacity, length * unit), BF16), vmem((2, 2 * capacity, wide), BF16),
            dma((2, groups * length + 3)),
        ]
    else:
        scratch += [
            vmem((2, width, 2 * capacity), BF16),
            vmem((length, unit, wide), BF16), vmem((length, unit, wide), BF16),
        ]
    found = pl.pallas_call(
        functools.partial(layer_kernel, groups, blocks, min(256, tokens), direct),
        in_specs=[whole] * 4 + [away] * 7,
        out_specs=[away] * 4 + [whole] + [away] * 2,
        out_shape=[
            flat, flat, flat, jax.ShapeDtypeStruct((rows, width), BF16), jax.ShapeDtypeStruct((1, rows), BF16),
            jax.ShapeDtypeStruct((unit, wide), F32), jax.ShapeDtypeStruct((unit_down, width), F32),
        ],
        scratch_shapes=scratch,
        compiler_params=pltpu.CompilerParams(
            collective_id=0, has_side_effects=True, vmem_limit_bytes=67043328
        ),
        name="layer",
    )(
        expert_ids.reshape(1, rows), router_gates.reshape(1, rows), moe_in, grad_out, w_gate_up[0], w_down[0], w_out,
        attn_query, attn_key, attn_value, prefix_state[0],
    )
    dquery, dkey, dvalue, resid, dgates, up, down = pass_on(*found)
    return dquery, dkey, dvalue, resid, dgates.reshape(rows, 1), up, down


def on_device(*args):
    dquery, dkey, dvalue, resid, dgates, up, down = compute(*args)
    return dquery, dkey, dvalue, resid, dgates, up[None], down[None]


def solution(mesh):
    return jax.shard_map(
        on_device,
        mesh=mesh,
        in_specs=(
            P("ctx", "exp"),
            P("ctx", "exp"),
            P("ctx", "exp"),
            P("ctx", "exp", None, None),
            P(("ctx", "exp"), None),
            P(("ctx", "exp"), None),
            P(("ctx", "exp"), None),
            P(("ctx", "exp"), None),
            P("exp", None, None),
            P("exp", None, None),
            P("exp", None),
        ),
        out_specs=(
            P("ctx", "exp"),
            P("ctx", "exp"),
            P("ctx", "exp"),
            P(("ctx", "exp"), None),
            P(("ctx", "exp"), None),
            P("exp", "ctx", None),
            P("exp", "ctx", None),
        ),
        check_vma=False,
    )
```

time: 182 us -> 130 us (0.71); the launches traced: 182 us -> 128 us
  Pallas kernels: 169 us -> 127 us
  local copies, waits for them, and re-layouts: 9.95 us -> 0 us
  other arithmetic: 2.25 us -> 0 us
    pallas_call x1, Pallas kernels: 169 us -> 122 us  [compute(): pl.pallas_call(functools.partial(layer_kernel, groups, blocks, min(256, t...]
    unnamed x17 -> x0, local copies, waits for them, and re-layouts: 8.62 us -> none
    pallas_call x0 -> x1, Pallas kernels: none -> 5.55 us  [pass_on(): pl.pallas_call(pass_kernel, grid=(steps,), in_specs=specs, out_specs=spec...]
where the time goes in v1:
time: 130 us; the launch traced here: 128 us
  Pallas kernels  127 us (98%)
    pallas_call x1, Pallas kernels, compute(): pl.pallas_call(functools.partial(layer_kernel, groups, blocks, min(256, t...  122 us
    pallas_call x1, Pallas kernels, pass_on(): pl.pallas_call(pass_kernel, grid=(steps,), in_specs=specs, out_specs=spec...  5.55 us

profile of v1, /device:TPU:16, one launch (start us, length us, event | category | flops | bytes accessed | tf_op | source)
XLA Modules:
  0.0 128.1 jit_solution(6045359816140823858)
XLA Ops:
  0.6 121.7 %layer.1 = (bf16[1024,512]{1,0:T(8,128)(2,1)}, bf16[1024,512]{1,0:T(8,128)(2,1)}, bf16[1024,512]{1,0:T(8,128)(2,1)}, bf16[256,2048]{1,0:T(8,128)(2,1)}, bf16[1,2...) custom-call(s32[1,256]{1,0:T(1,128)} %bitcast.11, bf16[1,256]{1,0:T(2,128)(2,1)} %bitcast.12, ...), custom_call_target="tpu_custom_call" | custom-call | tf_op jit(solution)/shard_map/layer/pallas_call | solution.py:563
  122.4 5.5 %pass_on.1 = (bf16[1024,512]{1,0:T(8,128)(2,1)}, bf16[1024,512]{1,0:T(8,128)(2,1)}, bf16[1024,512]{1,0:T(8,128)(2,1)}, bf16[256,2048]{1,0:T(8,128)(2,1)}, bf16[1...) custom-call(bf16[1024,512]{1,0:T(8,128)(2,1)} %get-tuple-element.21.refs_0_, ...), custom_call_target="tpu_custom_call" | custom-call | tf_op jit(solution)/shard_map/pass_on/pallas_call | solution.py:500

commit v2 on v1

--- a/solution.py
+++ b/solution.py
@@ -71,17 +71,17 @@
         dquery_hbm, dkey_hbm, dvalue_hbm, resid_hbm, dgates_ref, up_hbm, down_hbm,
         pair_ref, back_ref, proj_ref, query_ref, key_ref, value_ref, prior_ref, load_sem,
         dquery_ref, dkey_ref, dvalue_ref, resid_ref, up_ref, down_ref, store_sem,
-        targets_ref, target_sem, packed_ref, came_ref, token_sem,
+        targets_ref, target_sem, packed_ref, came_ref, gate_packed_ref, gate_came_ref, token_sem,
         scaled_ref, both_ref, hidden_t_ref, gate_out_ref, gate_in_ref, gate_sem,
         rows_ref, rows_sem, slots_ref, grad_ref, scaled_grad_ref,
-        local_ref, later_ref, line_ref, state_out_ref, state_in_ref, state_sem,
+        local_ref, line_ref, state_out_ref, state_in_ref, state_sem,
         pair_down_out, pair_down_in, pair_sem,
         line_up_out, line_up_in, line_down_out, line_down_in, line_sem,
-    ) = refs[:63]
+    ) = refs[:64]
     if direct:
-        other_rows_ref, other_both_ref, other_sem = refs[63:]
+        other_rows_ref, other_both_ref, other_sem = refs[64:]
     else:
-        rows_t_ref, pair_up_out, pair_up_in = refs[63:]
+        rows_t_ref, pair_up_out, pair_up_in = refs[64:]
     me, block = lax.axis_index("exp"), lax.axis_index("ctx")
     side, place = lax.rem(block, 2), lax.div(block, 2)
     length = blocks // 2
@@ -138,6 +138,17 @@
         spots = lax.broadcasted_iota(jnp.int32, (capacity, tokens_own), 0) + expert * capacity
         return jnp.where(spots == targets, 1.0, 0.0)
 
+    eye = jnp.where(
+        lax.broadcasted_iota(jnp.int32, (capacity, LANES), 0) == lax.broadcasted_iota(jnp.int32, (capacity, LANES), 1),
+        1.0, 0.0,
+    )
+
+    def as_row(column):
+        return jnp.broadcast_to(jnp.sum(eye * column, axis=0, keepdims=True), (16, LANES)).astype(BF16)
+
+    def as_column(rows):
+        return jnp.sum(eye * rows[0:1, :].astype(F32), axis=1, keepdims=True)
+
     token_copies, target_copies = {}, {}
     for k in (2, 3, 1, 0):
         found = placing(flipped(me, k), own_target)
@@ -145,8 +156,8 @@
         out = packed_ref.at[k - 1] if k else came_ref.at[0]
         out[:, :width] = plain(chosen, moe_ref[...]).astype(BF16)
         out[:, width : 2 * width] = plain(chosen, cot_ref[...]).astype(BF16)
-        gate = jnp.sum(found * gates_row, axis=1, keepdims=True)
-        out[:, 2 * width :] = jnp.broadcast_to(gate, (capacity, LANES)).astype(BF16)
+        gate_out = gate_packed_ref.at[k - 1] if k else gate_came_ref.at[0]
+        gate_out[...] = as_row(jnp.sum(found * gates_row, axis=1, keepdims=True))
         if k == 2:
             pl.semaphore_wait(barrier, len(peers))
         if k:
@@ -154,8 +165,11 @@
                 sends.start(
                     out.at[:, cols], came_ref.at[k, :, cols], token_sem.at[0, k, half], token_sem.at[1, k, half], near(k)
                 )
-                for half, cols in enumerate((pl.ds(0, width), pl.ds(width, width + LANES)))
+                for half, cols in enumerate((pl.ds(0, width), pl.ds(width, width)))
             ]
+            token_copies[k].append(
+                sends.start(gate_out, gate_came_ref.at[k], token_sem.at[0, k, 2], token_sem.at[1, k, 2], near(k))
+            )
     for k in range(1, groups):
         target_copies[k] = sends.start(
             targets_ref.at[0], targets_ref.at[k], target_sem.at[0, k], target_sem.at[1, k], near(k)
@@ -189,8 +203,9 @@
         for k in which:
             if k:
                 token_copies[k][1].wait_recv()
+                token_copies[k][2].wait_recv()
         cot = jnp.concatenate([came_ref[k, :, width : 2 * width] for k in which], axis=0).astype(F32)
-        gate = jnp.concatenate([came_ref[k, :, 2 * width :] for k in which], axis=0)[:, :1].astype(F32)
+        gate = jnp.concatenate([as_column(gate_came_ref[k]) for k in which], axis=0)
         scaled = (gate * cot).astype(BF16)
         scaled_ref[part, inner, :] = scaled
         grad_hidden = contract_cols(scaled, back_ref[...])
@@ -209,14 +224,14 @@
         output = plain(hidden, back_ref[...])
         grad_gate = jnp.sum(cot * output, axis=1, keepdims=True)
         for spot, k in enumerate(which):
-            one = jnp.broadcast_to(grad_gate[spot * capacity : (spot + 1) * capacity], (capacity, LANES))
+            one = as_row(grad_gate[spot * capacity : (spot + 1) * capacity])
             if k:
-                gate_out_ref[k - 1] = one.astype(BF16)
+                gate_out_ref[k - 1] = one
                 gate_copies[k] = sends.start(
                     gate_out_ref.at[k - 1], gate_in_ref.at[k], gate_sem.at[0, k], gate_sem.at[1, k], near(k)
                 )
             else:
-                gate_in_ref[0] = one.astype(BF16)
+                gate_in_ref[0] = one
         return hidden
 
     pieces = [pl.ds(0, 2 * capacity), pl.ds(2 * capacity, capacity), pl.ds(3 * capacity, capacity)]
@@ -351,11 +366,11 @@
     project_near(2)
     for copy in other_copies:
         copy.wait_recv()
-    ends((0, 0), (0, 1))
+    ends((0, 0), (1, 0), (0, 1), (1, 1))
     project_far(0)
     middles((0, 0))
     project_far(1)
-    ends((1, 0))
+    middles((1, 0))
     project_far(2)
 
     base = (3 * blocks + block) * tokens
@@ -385,9 +400,40 @@
             state = contract_rows(query_ref[at, cols], scaled[:, cols])
             local_ref[h] = state + local_ref[h] if i else state
 
-    state_out_ref[0] = local_ref[...].astype(BF16)
-    pair_state = sends.start(state_out_ref.at[0], state_in_ref.at[0], state_sem.at[0, 0], state_sem.at[1, 0], partner)
-    middles((0, 1))
+    steps, step = [], 1
+    while step < length:
+        steps.append(step)
+        step *= 2
+
+    def state_copy(turn, device):
+        return pltpu.make_async_remote_copy(
+            src_ref=state_out_ref.at[turn], dst_ref=state_in_ref.at[turn], send_sem=state_sem.at[0, turn],
+            recv_sem=state_sem.at[1, turn], device_id=device, device_id_type=MESH,
+        )
+
+    last = at_least(place, length - 1, 2 * length)
+
+    def send_state(turn, chosen):
+        @pl.when((place >= steps[turn]) & (chosen == 1))
+        def _():
+            value = local_ref[...] + line_ref[...] if turn else local_ref[...]
+            state_out_ref[turn] = value.astype(BF16)
+            state_copy(turn, {"ctx": lax.rem(block + blocks - 2 * steps[turn], blocks)}).start()
+
+    def take_state(turn):
+        @pl.when(place + steps[turn] < length)
+        def _():
+            state_copy(turn, partner).wait_recv()
+            line_ref[...] += state_in_ref[turn].astype(F32)
+
+    line_ref[...] = jnp.zeros_like(line_ref)
+    if steps:
+        send_state(0, 1)
+    for turn in range(1, len(steps)):
+        send_state(turn, last)
+    for j in range(2, length - 1):
+        ends((0, j), (1, j))
+    middles((1, 1), (0, 1), (1, 2))
 
     own = jnp.concatenate([placing(flipped(me, j), own_target).astype(BF16) for j in range(groups)], axis=0)
     rows = jnp.concatenate([rows_ref[j, j * capacity : (j + 1) * capacity, :] for j in range(groups)], axis=0)
@@ -395,33 +441,11 @@
     store(resid_ref, resid_hbm)
     for k in range(1, groups):
         gate_copies[k].wait_recv()
-    gates = jnp.concatenate([gate_in_ref[k] for k in range(groups)], axis=0)
-    dgates_ref[...] = contract_rows(gates, own)[0:1, :].astype(BF16)
-
-    pair_state.wait_recv()
-    local_ref[...] = local_ref[...] + state_in_ref[0].astype(F32)
-    later_ref[...] = state_in_ref[0].astype(F32) * (1 - side).astype(F32)
-    line_ref[...] = jnp.zeros_like(line_ref)
-    turn, step, steps = 1, 1, []
-    while step < length:
-        steps.append((turn, step))
-        turn, step = turn + 1, 2 * step
-
-    def send_state(turn, step):
-        state_out_ref[turn] = (local_ref[...] + line_ref[...]).astype(BF16)
-        sends.start(
-            state_out_ref.at[turn], state_in_ref.at[turn], state_sem.at[0, turn], state_sem.at[1, turn],
-            {"ctx": lax.rem(block + blocks - 2 * step, blocks)}, when=place >= step,
-        )
-
-    def take_state(turn, step):
-        @pl.when(place + step < length)
-        def _():
-            pltpu.make_async_remote_copy(
-                src_ref=state_in_ref.at[turn], dst_ref=state_in_ref.at[turn], send_sem=state_sem.at[0, turn],
-                recv_sem=state_sem.at[1, turn], device_id=partner, device_id_type=MESH,
-            ).wait_recv()
-            line_ref[...] += state_in_ref[turn].astype(F32)
+    gates = None
+    for k in range(groups):
+        one = plain(gate_in_ref[k, :, :capacity], placing(flipped(me, k), own_target).astype(BF16))
+        gates = one if gates is None else gates + one
+    dgates_ref[...] = gates[0:1, :].astype(BF16)
 
     row = lax.broadcasted_iota(jnp.int32, (chunk, chunk), 0)
     col = lax.broadcasted_iota(jnp.int32, (chunk, chunk), 1)
@@ -440,7 +464,7 @@
 
     def backward(h, carry):
         cols = pl.ds(pl.multiple_of(h * head_dim, head_dim), head_dim)
-        state = later_ref[h] + line_ref[h]
+        state = line_ref[h]
         for at in reversed(range(tokens // chunk)):
             rows = pl.ds(at * chunk, chunk)
             query, keys = query_ref[rows, cols], key_ref[rows, cols]
@@ -454,20 +478,24 @@
         return carry
 
     loads[6].wait()
-    if steps:
-        send_state(*steps[0])
-    for j in range(2, length - 1):
-        line_item(0, j)
-    lax.fori_loop(0, heads, forward, 0)
-    store(dquery_ref, dquery_hbm)
-    for at, one in enumerate(steps):
-        if at:
-            send_state(*one)
-            if at == 1:
-                middles((1, 0))
-                for j in range(1, length - 1):
-                    line_item(1, j)
-        take_state(*one)
+    for turn in range(len(steps)):
+        take_state(turn)
+        if turn + 1 < len(steps):
+            send_state(turn + 1, 1 - last)
+        if turn == 0:
+            middles((0, 2))
+            for j in range(3, length - 1):
+                middles((1, j), (0, j))
+            lax.fori_loop(0, heads, forward, 0)
+            store(dquery_ref, dquery_hbm)
+    if not steps:
+        lax.fori_loop(0, heads, forward, 0)
+        store(dquery_ref, dquery_hbm)
+    across = len(steps)
+    state_out_ref[across] = (line_ref[...] + local_ref[...] * side.astype(F32)).astype(BF16)
+    state_copy(across, partner).start()
+    state_copy(across, partner).wait_recv()
+    line_ref[...] += state_in_ref[across].astype(F32)
     lax.fori_loop(0, heads, backward, 0)
     store(dkey_ref, dkey_hbm)
     store(dvalue_ref, dvalue_hbm)
@@ -480,29 +508,39 @@
     for kind in range(2):
         for j in range(length - 1):
             line_copy(kind, j, 0, partner).wait_send()
+    for turn in range(len(steps)):
+
+        @pl.when(place >= steps[turn])
+        def _():
+            state_copy(turn, partner).wait_send()
+
+    state_copy(across, partner).wait_send()
     sends.drain()
 
 
-def pass_kernel(*refs):
-    half = len(refs) // 2
-    for src, dst in zip(refs[:half], refs[half:]):
-        dst[...] = src[...]
+def pass_kernel(count, *refs):
+    sources, targets, held, sems = refs[:count], refs[count : 2 * count], refs[2 * count : 3 * count], refs[3 * count]
+    into, out_of = [], []
+    for at in range(count):
+        into.append(pltpu.make_async_copy(sources[at], held[at], sems.at[0, at]))
+        into[-1].start()
+    for at in range(count):
+        into[at].wait()
+        out_of.append(pltpu.make_async_copy(held[at], targets[at], sems.at[1, at]))
+        out_of[-1].start()
+    for copy in out_of:
+        copy.wait()
 
 
 def pass_on(*arrays):
-    steps = 4
-    specs = [
-        pl.BlockSpec(one.shape, lambda i: (0, 0))
-        if one.shape[0] % (16 * steps)
-        else pl.BlockSpec((one.shape[0] // steps, one.shape[1]), lambda i: (i, 0))
-        for one in arrays
-    ]
+    away = [pl.BlockSpec(memory_space=pl.ANY)] * len(arrays)
     return pl.pallas_call(
-        pass_kernel,
-        grid=(steps,),
-        in_specs=specs,
-        out_specs=specs,
+        functools.partial(pass_kernel, len(arrays)),
+        in_specs=away,
+        out_specs=away,
         out_shape=[jax.ShapeDtypeStruct(one.shape, one.dtype) for one in arrays],
+        scratch_shapes=[pltpu.VMEM(one.shape, one.dtype) for one in arrays]
+        + [pltpu.SemaphoreType.DMA((2, len(arrays)))],
         name="pass_on",
     )(*arrays)
 
@@ -534,15 +572,15 @@
         flat_ref, flat_ref, flat_ref, vmem((rows, width), BF16), vmem((unit, wide), F32),
         vmem((unit_down, width), F32), dma((6,)),
         vmem((groups, 8, rows), jnp.int32), dma((2, groups)),
-        vmem((groups - 1, capacity, 2 * width + LANES), BF16),
-        vmem((groups, capacity, 2 * width + LANES), BF16), dma((2, groups, 2)),
+        vmem((groups - 1, capacity, 2 * width), BF16), vmem((groups, capacity, 2 * width), BF16),
+        vmem((groups - 1, 16, LANES), BF16), vmem((groups, 16, LANES), BF16), dma((2, groups, 3)),
         vmem((2, 2 * capacity, width), BF16), vmem((2, 2 * capacity, wide), BF16),
         vmem((2, hidden_units, 2 * capacity), BF16),
-        vmem((groups - 1, capacity, LANES), BF16), vmem((groups, capacity, LANES), BF16), dma((2, groups)),
+        vmem((groups - 1, 16, LANES), BF16), vmem((groups, 16, LANES), BF16), dma((2, groups)),
         vmem((groups, groups * capacity, width), BF16), dma((2, groups, 3)),
         vmem((groups, groups * capacity, cols), BF16),
         flat_ref, flat_ref,
-        state, state, state,
+        state, state,
         vmem((turns, heads, head_dim, head_dim), BF16), vmem((turns, heads, head_dim, head_dim), BF16),
         dma((2, turns)),
         vmem((length, unit_down, width), BF16), vmem((length, unit_down, width), BF16), dma((2, 2, length)),

time: 130 us -> 118 us (0.908)
  the two profiles are of different devices: /device:TPU:16 before, /device:TPU:12 now
where the time goes in v2:
time: 118 us
  Pallas kernels  117 us (99%)
    pallas_call x1, Pallas kernels, compute(): pl.pallas_call(functools.partial(layer_kernel, groups, blocks, min(256, t...  112 us
    pallas_call x1, Pallas kernels, pass_on(): pl.pallas_call(functools.partial(pass_kernel, len(arrays)), in_specs=away...  4.77 us

profile of v2, /device:TPU:12, one launch (start us, length us, event | category | flops | bytes accessed | tf_op | source)
XLA Modules:
  0.0 117.5 jit_solution(8796163321160665108)
XLA Ops:
  0.6 111.9 %layer.1 = (bf16[1024,512]{1,0:T(8,128)(2,1)}, bf16[1024,512]{1,0:T(8,128)(2,1)}, bf16[1024,512]{1,0:T(8,128)(2,1)}, bf16[256,2048]{1,0:T(8,128)(2,1)}, bf16[1,2...) custom-call(s32[1,256]{1,0:T(1,128)} %bitcast.11, bf16[1,256]{1,0:T(2,128)(2,1)} %bitcast.12, ...), custom_call_target="tpu_custom_call" | custom-call | tf_op jit(solution)/shard_map/layer/pallas_call | solution.py:601
  112.6 4.8 %pass_on.1 = (bf16[1024,512]{1,0:T(8,128)(2,1)}, bf16[1024,512]{1,0:T(8,128)(2,1)}, bf16[1024,512]{1,0:T(8,128)(2,1)}, bf16[256,2048]{1,0:T(8,128)(2,1)}, bf16[1...) custom-call(bf16[1024,512]{1,0:T(8,128)(2,1)} %get-tuple-element.21.refs_0_, ...), custom_call_target="tpu_custom_call" | custom-call | tf_op jit(solution)/shard_map/pass_on/pallas_call | solution.py:537

commit v3 on v2

--- a/solution.py
+++ b/solution.py
@@ -67,21 +67,20 @@
 
 def layer_kernel(groups, blocks, chunk, direct, *refs):
     (
-        ids_ref, gates_ref, moe_ref, cot_ref, pair_hbm, back_hbm, proj_hbm, query_hbm, key_hbm, value_hbm, prior_hbm,
-        dquery_hbm, dkey_hbm, dvalue_hbm, resid_hbm, dgates_ref, up_hbm, down_hbm,
-        pair_ref, back_ref, proj_ref, query_ref, key_ref, value_ref, prior_ref, load_sem,
-        dquery_ref, dkey_ref, dvalue_ref, resid_ref, up_ref, down_ref, store_sem,
+        ids_ref, gates_ref, moe_hbm, cot_hbm, pair_hbm, back_hbm, proj_hbm, query_hbm, key_hbm, value_hbm, prior_hbm,
+        dquery_ref, dkey_ref, dvalue_ref, resid_ref, dgates_ref, up_ref, down_ref,
+        moe_ref, cot_ref, pair_ref, back_ref, proj_ref, query_ref, key_ref, value_ref, prior_ref, load_sem,
         targets_ref, target_sem, packed_ref, came_ref, gate_packed_ref, gate_came_ref, token_sem,
         scaled_ref, both_ref, hidden_t_ref, gate_out_ref, gate_in_ref, gate_sem,
         rows_ref, rows_sem, slots_ref, grad_ref, scaled_grad_ref,
         local_ref, line_ref, state_out_ref, state_in_ref, state_sem,
         pair_down_out, pair_down_in, pair_sem,
         line_up_out, line_up_in, line_down_out, line_down_in, line_sem,
-    ) = refs[:64]
+    ) = refs[:57+2]
     if direct:
-        other_rows_ref, other_both_ref, other_sem = refs[64:]
+        other_rows_ref, other_both_ref, other_sem = refs[57+2:]
     else:
-        rows_t_ref, pair_up_out, pair_up_in = refs[64:]
+        rows_t_ref, pair_up_out, pair_up_in = refs[57+2:]
     me, block = lax.axis_index("exp"), lax.axis_index("ctx")
     side, place = lax.rem(block, 2), lax.div(block, 2)
     length = blocks // 2
@@ -94,21 +93,6 @@
     partner = {"ctx": block + 1 - 2 * side}
     sends = Sends()
 
-    loads = []
-    for at, (src, dst) in enumerate(
-        [
-            (pair_hbm, pair_ref), (back_hbm, back_ref), (proj_hbm, proj_ref), (query_hbm, query_ref),
-            (key_hbm, key_ref), (value_hbm, value_ref), (prior_hbm, prior_ref),
-        ]
-    ):
-        loads.append(pltpu.make_async_copy(src, dst, load_sem.at[at]))
-        loads[-1].start()
-    stores = []
-
-    def store(src, dst):
-        stores.append(pltpu.make_async_copy(src, dst, store_sem.at[len(stores)]))
-        stores[-1].start()
-
     barrier = pltpu.get_barrier_semaphore()
     peers = [{"exp": flipped(me, k)} for k in range(1, groups)]
     shifts = [1]
@@ -119,6 +103,15 @@
     for peer in peers:
         pl.semaphore_signal(barrier, inc=1, device_id=peer, device_id_type=MESH)
 
+    loads = []
+    for at, (src, dst) in enumerate(
+        [
+            (moe_hbm, moe_ref), (cot_hbm, cot_ref), (pair_hbm, pair_ref), (back_hbm, back_ref), (proj_hbm, proj_ref), (query_hbm, query_ref),
+            (key_hbm, key_ref), (value_hbm, value_ref), (prior_hbm, prior_ref),
+        ]
+    ):
+        loads.append(pltpu.make_async_copy(src, dst, load_sem.at[at]))
+        loads[-1].start()
     def near(k):
         return {"exp": flipped(me, k)}
 
@@ -149,7 +142,10 @@
     def as_column(rows):
         return jnp.sum(eye * rows[0:1, :].astype(F32), axis=1, keepdims=True)
 
-    token_copies, target_copies = {}, {}
+    half = capacity // 2
+    token_copies, target_copies, gate_copies_in = {}, {}, {}
+    loads[0].wait()
+    loads[1].wait()
     for k in (2, 3, 1, 0):
         found = placing(flipped(me, k), own_target)
         chosen = found.astype(BF16)
@@ -161,39 +157,46 @@
         if k == 2:
             pl.semaphore_wait(barrier, len(peers))
         if k:
-            token_copies[k] = [
-                sends.start(
-                    out.at[:, cols], came_ref.at[k, :, cols], token_sem.at[0, k, half], token_sem.at[1, k, half], near(k)
+            token_copies[k] = []
+            cuts = [(0, capacity, 0)]
+            cuts += [(0, half, width), (half, half, width)] if k == 3 else [(0, capacity, width)]
+            for at, (begin, size, first) in enumerate(cuts):
+                spots, cols = pl.ds(begin, size), pl.ds(first, width)
+                if at == 1:
+                    gate_copies_in[k] = sends.start(
+                        gate_out, gate_came_ref.at[k], token_sem.at[0, k, 3], token_sem.at[1, k, 3], near(k)
+                    )
+                token_copies[k].append(
+                    sends.start(
+                        out.at[spots, cols], came_ref.at[k, spots, cols], token_sem.at[0, k, at],
+                        token_sem.at[1, k, at], near(k),
+                    )
                 )
-                for half, cols in enumerate((pl.ds(0, width), pl.ds(width, width)))
-            ]
-            token_copies[k].append(
-                sends.start(gate_out, gate_came_ref.at[k], token_sem.at[0, k, 2], token_sem.at[1, k, 2], near(k))
-            )
     for k in range(1, groups):
         target_copies[k] = sends.start(
             targets_ref.at[0], targets_ref.at[k], target_sem.at[0, k], target_sem.at[1, k], near(k)
         )
 
-    gate_copies, row_copies, relay_copies = {}, {}, {}
+    gate_copies, row_copies, relay_copies, kept = {}, {}, {}, []
     other_copies = []
 
     def other(src, dst):
         at = len(other_copies)
         other_copies.append(sends.start(src, dst, other_sem.at[0, at], other_sem.at[1, at], partner))
 
-    def expert(which, part, begin, piece):
-        size = len(which) * capacity
-        inner = pl.ds(begin, size)
+    def expert(which, part, begin, piece, rows=(0, capacity), turn=0):
+        spots_in = pl.ds(*rows)
+        size = len(which) * rows[1]
+        inner = pl.ds(begin + rows[0], size)
         for spot, k in enumerate(which):
-            if k:
+            if k and not turn:
                 token_copies[k][0].wait_recv()
-            if direct:
+            if direct and not turn:
                 for home in range(length):
                     cols = pl.ds(pl.multiple_of((2 * home + 1 - side) * unit, unit), unit)
                     spots = pl.ds(begin + spot * capacity, capacity)
                     other(came_ref.at[k, :, cols], other_rows_ref.at[part, spots, pl.ds(home * unit, unit)])
-        rows_in = jnp.concatenate([came_ref[k, :, :width] for k in which], axis=0)
+        rows_in = jnp.concatenate([came_ref[k, spots_in, :width] for k in which], axis=0)
         both = plain(rows_in, pair_ref[...])
         first, second = both[:, :hidden_units], both[:, hidden_units:]
         logistic = jax.nn.sigmoid(first)
@@ -202,10 +205,11 @@
         slope = logistic * (1.0 + first * (1.0 - logistic))
         for k in which:
             if k:
-                token_copies[k][1].wait_recv()
-                token_copies[k][2].wait_recv()
-        cot = jnp.concatenate([came_ref[k, :, width : 2 * width] for k in which], axis=0).astype(F32)
-        gate = jnp.concatenate([as_column(gate_came_ref[k]) for k in which], axis=0)
+                if not turn:
+                    gate_copies_in[k].wait_recv()
+                token_copies[k][1 + turn].wait_recv()
+        cot = jnp.concatenate([came_ref[k, spots_in, width : 2 * width] for k in which], axis=0).astype(F32)
+        gate = jnp.concatenate([as_column(gate_came_ref[k])[rows[0] : rows[0] + rows[1]] for k in which], axis=0)
         scaled = (gate * cot).astype(BF16)
         scaled_ref[part, inner, :] = scaled
         grad_hidden = contract_cols(scaled, back_ref[...])
@@ -214,16 +218,22 @@
         if direct:
             other(both_ref.at[part, inner], other_both_ref.at[part, inner])
         grad_rows = contract_cols(both_ref[part, inner, :], pair_ref[...]).astype(BF16)
-        at = pl.ds(part * 2 * capacity + begin, size)
+        at = pl.ds(part * 2 * capacity + begin + rows[0], size)
         rows_ref[0, at, :] = (cot + grad_rows.astype(F32)).astype(BF16)
-        for peer in (2, 1):
+        at = pl.ds(part * 2 * capacity + begin, len(which) * capacity)
+        done = rows[0] + rows[1] == capacity
+        for peer in (2, 1) if done else ():
             row_copies[peer, piece] = sends.start(
                 rows_ref.at[0, at], rows_ref.at[peer, at],
                 rows_sem.at[0, peer, piece], rows_sem.at[1, peer, piece], near(peer),
             )
         output = plain(hidden, back_ref[...])
         grad_gate = jnp.sum(cot * output, axis=1, keepdims=True)
-        for spot, k in enumerate(which):
+        if kept:
+            grad_gate = jnp.concatenate([kept.pop(), grad_gate], axis=0)
+        if not done:
+            kept.append(grad_gate)
+        for spot, k in enumerate(which) if done else ():
             one = as_row(grad_gate[spot * capacity : (spot + 1) * capacity])
             if k:
                 gate_out_ref[k - 1] = one
@@ -254,35 +264,41 @@
         relay_copies[piece].wait_recv()
         project(3, piece)
 
-    loads[0].wait()
-    loads[1].wait()
+    loads[2].wait()
+    loads[3].wait()
     hidden_t_ref[0] = expert((0, 1), 0, 0, 0).T
     if not direct:
         rows_t_ref[0] = jnp.concatenate([came_ref[0, :, :width], came_ref[1, :, :width]], axis=0).T
-    loads[2].wait()
+    loads[4].wait()
     project_near(0)
     hidden_2 = expert((2,), 1, 0, 1)
     project_near(1)
-    hidden_3 = expert((3,), 1, capacity, 2)
-    hidden_t_ref[1] = jnp.concatenate([hidden_2, hidden_3], axis=0).T
+    hidden_3 = expert((3,), 1, capacity, 2, (0, half))
+    hidden_4 = expert((3,), 1, capacity, 2, (half, half), 1)
+    hidden_t_ref[1] = jnp.concatenate([hidden_2, hidden_3, hidden_4], axis=0).T
     if not direct:
         rows_t_ref[1] = jnp.concatenate([came_ref[2, :, :width], came_ref[3, :, :width]], axis=0).T
 
-    def up_rows(which):
+    wide = both_ref.shape[2]
+    columns = {0: pl.ds(0, wide // 2), 2: pl.ds(wide // 2, wide // 2)}
+
+    def up_rows(which, over):
         at = pl.ds(pl.multiple_of(which * unit, unit), unit)
-        return plain(rows_t_ref[0, at, :], both_ref[0]) + plain(rows_t_ref[1, at, :], both_ref[1])
-
-    def up_pair(j, home):
+        return plain(rows_t_ref[0, at, :], both_ref[0, :, over]) + plain(rows_t_ref[1, at, :], both_ref[1, :, over])
+
+    def up_pair(kind, j, home):
+        over = columns[kind]
         if not direct:
-            pair_copies[0, j].wait_recv()
-            return up_rows(2 * home + side) + pair_up_in[j].astype(F32)
+            if kind == 0:
+                pair_copies[0, j].wait_recv()
+            return up_rows(2 * home + side, over) + pair_up_in[j, :, over].astype(F32)
         cols = pl.ds(pl.multiple_of((2 * home + side) * unit, unit), unit)
         there = pl.ds(pl.multiple_of(home * unit, unit), unit)
         found = None
         for part in range(2):
             here = jnp.concatenate([came_ref[2 * part, :, cols], came_ref[2 * part + 1, :, cols]], axis=0)
-            one = contract_rows(here, both_ref[part])
-            one = one + contract_rows(other_rows_ref[part, :, there], other_both_ref[part])
+            one = contract_rows(here, both_ref[part, :, over])
+            one = one + contract_rows(other_rows_ref[part, :, there], other_both_ref[part, :, over])
             found = one if found is None else found + one
         return found
 
@@ -306,7 +322,7 @@
     def pair_sends():
         for j, (home, _) in enumerate(items):
             if not direct:
-                pair_up_out[j] = up_rows(2 * home + 1 - side).astype(BF16)
+                pair_up_out[j] = up_rows(2 * home + 1 - side, pl.ds(0, wide)).astype(BF16)
                 pair_copies[0, j] = sends.start(
                     pair_up_out.at[j], pair_up_in.at[j], pair_sem.at[0, 0, j], pair_sem.at[1, 0, j], partner
                 )
@@ -319,20 +335,24 @@
     inside = has_left * has_right
 
     def line_copy(kind, j, slot, device):
-        out, line_in = ((line_up_out, line_up_in), (line_down_out, line_down_in))[kind]
+        if kind == 1:
+            src, dst = line_down_out.at[j], line_down_in.at[slot]
+        else:
+            src, dst = line_up_out.at[j, :, columns[kind]], line_up_in.at[slot, :, columns[kind]]
         return pltpu.make_async_remote_copy(
-            src_ref=out.at[j], dst_ref=line_in.at[slot], send_sem=line_sem.at[0, kind, j],
-            recv_sem=line_sem.at[1, kind, slot], device_id=device, device_id_type=MESH,
+            src_ref=src, dst_ref=dst, send_sem=line_sem.at[0, kind, j], recv_sem=line_sem.at[1, kind, slot],
+            device_id=device, device_id_type=MESH,
         )
 
     def line_item(kind, j):
         home, rightward = items[j]
-        total, out, line_in = ((up_ref, line_up_out, line_up_in), (down_ref, line_down_out, line_down_in))[kind]
-        if kind:
+        if kind == 1:
+            over, total, out, line_in = slice(None), down_ref, line_down_out, line_down_in
             pair_copies[1, j].wait_recv()
             total[...] = down_rows(2 * home + side) + pair_down_in[j].astype(F32)
         else:
-            total[...] = up_pair(j, home)
+            over, total, out, line_in = columns[kind], up_ref, line_up_out, line_up_in
+            total[:, over] = up_pair(kind, j, home)
         if rightward is None:
             ways = [(has_left, place + 1), (has_right, place)]
         else:
@@ -342,39 +362,43 @@
             @pl.when(present == 1)
             def _():
                 line_copy(kind, 0, slot, partner).wait_recv()
-                total[...] += line_in[slot].astype(F32)
+                total[:, over] += line_in[slot, :, over].astype(F32)
 
         if rightward is not None:
-            out[j] = total[...].astype(BF16)
+            out[j, :, over] = total[:, over].astype(BF16)
             line_copy(kind, j, home + rightward, {"ctx": block + 4 * rightward - 2}).start()
 
-    def ends(*which):
+    def ends(*which, last=False):
         @pl.when(inside == 0)
         def _():
             for kind, j in which:
-                if j < length - 1:
+                if last or j < length - 1:
                     line_item(kind, j)
 
-    def middles(*which):
+    def middles(*which, last=False):
         @pl.when(inside == 1)
         def _():
             for kind, j in which:
-                if j < length - 1:
+                if last or j < length - 1:
                     line_item(kind, j)
 
     pair_sends()
-    project_near(2)
     for copy in other_copies:
         copy.wait_recv()
-    ends((0, 0), (1, 0), (0, 1), (1, 1))
+    ends((0, 0), (2, 0))
+    project_near(2)
+    ends((1, 0), (0, 1), (2, 1))
+    middles((0, 0), (2, 0))
     project_far(0)
-    middles((0, 0))
+    ends((1, 1))
+    middles((1, 0), (0, 1), (2, 1))
     project_far(1)
-    middles((1, 0))
+    middles((0, 2), (1, 1))
     project_far(2)
+    middles((2, 2))
 
     base = (3 * blocks + block) * tokens
-    for at in (3, 4, 5):
+    for at in (5, 6, 7):
         loads[at].wait()
 
     def inverse_counts(start, shape):
@@ -400,45 +424,33 @@
             state = contract_rows(query_ref[at, cols], scaled[:, cols])
             local_ref[h] = state + local_ref[h] if i else state
 
-    steps, step = [], 1
-    while step < length:
-        steps.append(step)
-        step *= 2
-
-    def state_copy(turn, device):
+    cuts = [(0, heads // 2), (heads // 2, heads - heads // 2)] if heads > 1 else [(0, heads)]
+
+    def state_copy(turn, at, device):
+        part = pl.ds(*cuts[at])
         return pltpu.make_async_remote_copy(
-            src_ref=state_out_ref.at[turn], dst_ref=state_in_ref.at[turn], send_sem=state_sem.at[0, turn],
-            recv_sem=state_sem.at[1, turn], device_id=device, device_id_type=MESH,
+            src_ref=state_out_ref.at[turn, part], dst_ref=state_in_ref.at[turn, part],
+            send_sem=state_sem.at[0, turn, at], recv_sem=state_sem.at[1, turn, at],
+            device_id=device, device_id_type=MESH,
         )
 
-    last = at_least(place, length - 1, 2 * length)
-
-    def send_state(turn, chosen):
-        @pl.when((place >= steps[turn]) & (chosen == 1))
+    line_ref[...] = jnp.zeros_like(line_ref)
+
+    def send_state(chosen, at):
+        @pl.when(chosen * has_left == 1)
         def _():
-            value = local_ref[...] + line_ref[...] if turn else local_ref[...]
-            state_out_ref[turn] = value.astype(BF16)
-            state_copy(turn, {"ctx": lax.rem(block + blocks - 2 * steps[turn], blocks)}).start()
-
-    def take_state(turn):
-        @pl.when(place + steps[turn] < length)
-        def _():
-            state_copy(turn, partner).wait_recv()
-            line_ref[...] += state_in_ref[turn].astype(F32)
-
-    line_ref[...] = jnp.zeros_like(line_ref)
-    if steps:
-        send_state(0, 1)
-    for turn in range(1, len(steps)):
-        send_state(turn, last)
+            part = pl.ds(*cuts[at])
+            state_out_ref[0, part] = (local_ref[part] + line_ref[part]).astype(BF16)
+            state_copy(0, at, {"ctx": lax.rem(block + blocks - 2, blocks)}).start()
+
+    for at in range(len(cuts)):
+        send_state(1 - has_right, at)
     for j in range(2, length - 1):
-        ends((0, j), (1, j))
-    middles((1, 1), (0, 1), (1, 2))
+        ends((0, j), (2, j), (1, j))
 
     own = jnp.concatenate([placing(flipped(me, j), own_target).astype(BF16) for j in range(groups)], axis=0)
     rows = jnp.concatenate([rows_ref[j, j * capacity : (j + 1) * capacity, :] for j in range(groups)], axis=0)
     resid_ref[...] = contract_rows(own, rows).astype(BF16)
-    store(resid_ref, resid_hbm)
     for k in range(1, groups):
         gate_copies[k].wait_recv()
     gates = None
@@ -477,72 +489,63 @@
             state = state + contract_rows(query, scaled)
         return carry
 
-    loads[6].wait()
-    for turn in range(len(steps)):
-        take_state(turn)
-        if turn + 1 < len(steps):
-            send_state(turn + 1, 1 - last)
-        if turn == 0:
-            middles((0, 2))
-            for j in range(3, length - 1):
-                middles((1, j), (0, j))
-            lax.fori_loop(0, heads, forward, 0)
-            store(dquery_ref, dquery_hbm)
-    if not steps:
-        lax.fori_loop(0, heads, forward, 0)
-        store(dquery_ref, dquery_hbm)
-    across = len(steps)
-    state_out_ref[across] = (line_ref[...] + local_ref[...] * side.astype(F32)).astype(BF16)
-    state_copy(across, partner).start()
-    state_copy(across, partner).wait_recv()
-    line_ref[...] += state_in_ref[across].astype(F32)
-    lax.fori_loop(0, heads, backward, 0)
-    store(dkey_ref, dkey_hbm)
-    store(dvalue_ref, dvalue_hbm)
-    line_item(0, length - 1)
-    store(up_ref, up_hbm)
-    line_item(1, length - 1)
-    store(down_ref, down_hbm)
-    for copy in stores:
-        copy.wait()
-    for kind in range(2):
+    loads[8].wait()
+    lax.fori_loop(0, heads, forward, 0)
+    for at, cut in enumerate(cuts):
+        part = pl.ds(*cut)
+
+        @pl.when(has_right == 1)
+        def _():
+            state_copy(0, at, partner).wait_recv()
+            line_ref[part] = state_in_ref[0, part].astype(F32)
+
+        send_state(has_right, at)
+        state_out_ref[1, part] = (line_ref[part] + local_ref[part] * side.astype(F32)).astype(BF16)
+        state_copy(1, at, partner).start()
+    middles((1, 2))
+    for j in range(3, length - 1):
+        middles((0, j), (2, j), (1, j))
+    finals = [(0, length - 1), (2, length - 1), (1, length - 1)]
+    ends(*finals, last=True)
+    for at, (begin, size) in enumerate(cuts):
+        part = pl.ds(begin, size)
+        state_copy(1, at, partner).wait_recv()
+        line_ref[part] += state_in_ref[1, part].astype(F32)
+        lax.fori_loop(begin, begin + size, backward, 0)
+    middles(*finals, last=True)
+    for kind in range(3):
         for j in range(length - 1):
             line_copy(kind, j, 0, partner).wait_send()
-    for turn in range(len(steps)):
-
-        @pl.when(place >= steps[turn])
+
+    for at in range(len(cuts)):
+
+        @pl.when(has_left == 1)
         def _():
-            state_copy(turn, partner).wait_send()
-
-    state_copy(across, partner).wait_send()
+            state_copy(0, at, partner).wait_send()
+
+        state_copy(1, at, partner).wait_send()
     sends.drain()
 
 
 def pass_kernel(count, *refs):
-    sources, targets, held, sems = refs[:count], refs[count : 2 * count], refs[2 * count : 3 * count], refs[3 * count]
-    into, out_of = [], []
-    for at in range(count):
-        into.append(pltpu.make_async_copy(sources[at], held[at], sems.at[0, at]))
-        into[-1].start()
-    for at in range(count):
-        into[at].wait()
-        out_of.append(pltpu.make_async_copy(held[at], targets[at], sems.at[1, at]))
-        out_of[-1].start()
-    for copy in out_of:
+    sems = refs[2 * count]
+    copies = [pltpu.make_async_copy(refs[at], refs[count + at], sems.at[at]) for at in range(count)]
+    for copy in copies:
+        copy.start()
+    for copy in copies:
         copy.wait()
 
 
 def pass_on(*arrays):
-    away = [pl.BlockSpec(memory_space=pl.ANY)] * len(arrays)
     return pl.pallas_call(
         functools.partial(pass_kernel, len(arrays)),
-        in_specs=away,
-        out_specs=away,
+        in_specs=[pl.BlockSpec(memory_space=pltpu.VMEM)] * len(arrays),
+        out_specs=[pl.BlockSpec(memory_space=pl.ANY)] * len(arrays),
         out_shape=[jax.ShapeDtypeStruct(one.shape, one.dtype) for one in arrays],
-        scratch_shapes=[pltpu.VMEM(one.shape, one.dtype) for one in arrays]
-        + [pltpu.SemaphoreType.DMA((2, len(arrays)))],
+        scratch_shapes=[pltpu.SemaphoreType.DMA((len(arrays),))],
+        compiler_params=pltpu.CompilerParams(vmem_limit_bytes=1 << 20),
         name="pass_on",
-    )(*arrays)
+    )(*[pltpu.with_memory_space_constraint(one, pltpu.VMEM) for one in arrays])
 
 
 def compute(
@@ -557,23 +560,21 @@
     tokens, cols = attn_query.shape
     heads, head_dim = prefix_state.shape[1:3]
     length = blocks // 2
-    turns = max(length.bit_length(), 1)
+    turns = 2
     direct = unit % LANES == 0
     whole = pl.BlockSpec(memory_space=pltpu.VMEM)
     away = pl.BlockSpec(memory_space=pl.ANY)
-    flat = jax.ShapeDtypeStruct((tokens, cols), BF16)
     dma = pltpu.SemaphoreType.DMA
     vmem = pltpu.VMEM
     state = vmem((heads, head_dim, head_dim), F32)
     flat_ref = vmem((tokens, cols), BF16)
     scratch = [
+        vmem((rows, width), BF16), vmem((rows, width), BF16),
         vmem((width, wide), BF16), vmem((hidden_units, width), BF16), vmem((cols, width), BF16),
-        flat_ref, flat_ref, flat_ref, state, dma((7,)),
-        flat_ref, flat_ref, flat_ref, vmem((rows, width), BF16), vmem((unit, wide), F32),
-        vmem((unit_down, width), F32), dma((6,)),
+        flat_ref, flat_ref, flat_ref, state, dma((9,)),
         vmem((groups, 8, rows), jnp.int32), dma((2, groups)),
         vmem((groups - 1, capacity, 2 * width), BF16), vmem((groups, capacity, 2 * width), BF16),
-        vmem((groups - 1, 16, LANES), BF16), vmem((groups, 16, LANES), BF16), dma((2, groups, 3)),
+        vmem((groups - 1, 16, LANES), BF16), vmem((groups, 16, LANES), BF16), dma((2, groups, 4)),
         vmem((2, 2 * capacity, width), BF16), vmem((2, 2 * capacity, wide), BF16),
         vmem((2, hidden_units, 2 * capacity), BF16),
         vmem((groups - 1, 16, LANES), BF16), vmem((groups, 16, LANES), BF16), dma((2, groups)),
@@ -582,16 +583,16 @@
         flat_ref, flat_ref,
         state, state,
         vmem((turns, heads, head_dim, head_dim), BF16), vmem((turns, heads, head_dim, head_dim), BF16),
-        dma((2, turns)),
+        dma((2, turns, 2)),
         vmem((length, unit_down, width), BF16), vmem((length, unit_down, width), BF16), dma((2, 2, length)),
         vmem((length - 1, unit, wide), BF16), vmem((length + 1, unit, wide), BF16),
         vmem((length - 1, unit_down, width), BF16), vmem((length + 1, unit_down, width), BF16),
-        dma((2, 2, length + 1)),
+        dma((2, 3, length + 1)),
     ]
     if direct:
         scratch += [
             vmem((2, 2 * capacity, length * unit), BF16), vmem((2, 2 * capacity, wide), BF16),
-            dma((2, groups * length + 3)),
+            dma((2, groups * length + 4)),
         ]
     else:
         scratch += [
@@ -600,15 +601,15 @@
         ]
     found = pl.pallas_call(
         functools.partial(layer_kernel, groups, blocks, min(256, tokens), direct),
-        in_specs=[whole] * 4 + [away] * 7,
-        out_specs=[away] * 4 + [whole] + [away] * 2,
+        in_specs=[whole] * 2 + [away] * 9,
+        out_specs=[whole] * 7,
         out_shape=[
-            flat, flat, flat, jax.ShapeDtypeStruct((rows, width), BF16), jax.ShapeDtypeStruct((1, rows), BF16),
-            jax.ShapeDtypeStruct((unit, wide), F32), jax.ShapeDtypeStruct((unit_down, width), F32),
+            flat_ref, flat_ref, flat_ref, vmem((rows, width), BF16), vmem((1, rows), BF16),
+            vmem((unit, wide), F32), vmem((unit_down, width), F32),
         ],
         scratch_shapes=scratch,
         compiler_params=pltpu.CompilerParams(
-            collective_id=0, has_side_effects=True, vmem_limit_bytes=67043328
+            collective_id=0, has_side_effects=True, vmem_limit_bytes=56000000
         ),
         name="layer",
     )(

time: 118 us -> 106 us (0.90)
  the two profiles are of different devices: /device:TPU:12 before, /device:TPU:16 now
where the time goes in v3:
time: 106 us; the launch traced here: 105 us
  Pallas kernels  104 us (98%)
    pallas_call x1, Pallas kernels, compute(): pl.pallas_call(functools.partial(layer_kernel, groups, blocks, min(256, t...  101 us
    pallas_call x1, Pallas kernels, pass_on(): pl.pallas_call(functools.partial(pass_kernel, len(arrays)), in_specs=[pl....  2.56 us

profile of v3, /device:TPU:16, one launch (start us, length us, event | category | flops | bytes accessed | tf_op | source)
XLA Modules:
  0.0 104.6 jit_solution(697395147207886293)
XLA Ops:
  0.6 101.2 %layer.1 = (bf16[1024,512]{1,0:T(8,128)(2,1)S(1)}, bf16[1024,512]{1,0:T(8,128)(2,1)S(1)}, bf16[1024,512]{1,0:T(8,128)(2,1)S(1)}, bf16[256,2048]{1,0:T(8,128)(2,1...) custom-call(s32[1,256]{1,0:T(1,128)} %bitcast.11, bf16[1,256]{1,0:T(2,128)(2,1)} %bitcast.12, ...), custom_call_target="tpu_custom_call" | custom-call | tf_op jit(solution)/shard_map/layer/pallas_call | solution.py:602
  101.8 2.6 %pass_on.1 = (bf16[1024,512]{1,0:T(8,128)(2,1)}, bf16[1024,512]{1,0:T(8,128)(2,1)}, bf16[1024,512]{1,0:T(8,128)(2,1)}, bf16[256,2048]{1,0:T(8,128)(2,1)}, bf16[1...) custom-call(bf16[1024,512]{1,0:T(8,128)(2,1)S(1)} %get-tuple-element.21.refs_0_, ...), custom_call_target="tpu_custom_call" | custom-call | tf_op jit(solution)/shard_map/pass_on/pallas_call | solution.py:540

commit v4 on v3

--- a/solution.py
+++ b/solution.py
@@ -58,7 +58,8 @@
         return copy
 
     def drain(self):
-        for copy, when in self.open:
+        pending, self.open = self.open, []
+        for copy, when in pending:
             if when is None:
                 copy.wait_send()
             else:
@@ -73,14 +74,14 @@
         targets_ref, target_sem, packed_ref, came_ref, gate_packed_ref, gate_came_ref, token_sem,
         scaled_ref, both_ref, hidden_t_ref, gate_out_ref, gate_in_ref, gate_sem,
         rows_ref, rows_sem, slots_ref, grad_ref, scaled_grad_ref,
-        local_ref, line_ref, state_out_ref, state_in_ref, state_sem,
+        local_ref, line_ref, later_ref, state_out_ref, state_in_ref, state_sem,
         pair_down_out, pair_down_in, pair_sem,
         line_up_out, line_up_in, line_down_out, line_down_in, line_sem,
-    ) = refs[:57+2]
+    ) = refs[:60]
     if direct:
-        other_rows_ref, other_both_ref, other_sem = refs[57+2:]
+        other_rows_ref, other_both_ref, other_sem = refs[60:]
     else:
-        rows_t_ref, pair_up_out, pair_up_in = refs[57+2:]
+        rows_t_ref, pair_up_out, pair_up_in = refs[60:]
     me, block = lax.axis_index("exp"), lax.axis_index("ctx")
     side, place = lax.rem(block, 2), lax.div(block, 2)
     length = blocks // 2
@@ -93,16 +94,6 @@
     partner = {"ctx": block + 1 - 2 * side}
     sends = Sends()
 
-    barrier = pltpu.get_barrier_semaphore()
-    peers = [{"exp": flipped(me, k)} for k in range(1, groups)]
-    shifts = [1]
-    while shifts[-1] < blocks // 2:
-        shifts.append(2 * shifts[-1])
-    for shift in shifts:
-        peers += [{"ctx": lax.rem(block + shift, blocks)}, {"ctx": lax.rem(block + blocks - shift, blocks)}]
-    for peer in peers:
-        pl.semaphore_signal(barrier, inc=1, device_id=peer, device_id_type=MESH)
-
     loads = []
     for at, (src, dst) in enumerate(
         [
@@ -111,7 +102,16 @@
         ]
     ):
         loads.append(pltpu.make_async_copy(src, dst, load_sem.at[at]))
-        loads[-1].start()
+    loads[0].start()
+    loads[1].start()
+    barrier = pltpu.get_barrier_semaphore()
+    peers = [{"exp": flipped(me, k)} for k in range(1, groups)]
+    shifts = (1, 2, 3)
+    for shift in shifts:
+        peers += [{"ctx": lax.rem(block + shift, blocks)}, {"ctx": lax.rem(block + blocks - shift, blocks)}]
+    for peer in peers:
+        pl.semaphore_signal(barrier, inc=1, device_id=peer, device_id_type=MESH)
+
     def near(k):
         return {"exp": flipped(me, k)}
 
@@ -142,36 +142,42 @@
     def as_column(rows):
         return jnp.sum(eye * rows[0:1, :].astype(F32), axis=1, keepdims=True)
 
-    half = capacity // 2
+    half = 2 * capacity // 3 // 16 * 16
     token_copies, target_copies, gate_copies_in = {}, {}, {}
     loads[0].wait()
-    loads[1].wait()
     for k in (2, 3, 1, 0):
         found = placing(flipped(me, k), own_target)
         chosen = found.astype(BF16)
         out = packed_ref.at[k - 1] if k else came_ref.at[0]
+        gate_out = gate_packed_ref.at[k - 1] if k else gate_came_ref.at[0]
+        token_copies[k] = []
+
+        def send_tokens(begin, size, first):
+            spots, cols, at = pl.ds(begin, size), pl.ds(first, width), len(token_copies[k])
+            token_copies[k].append(
+                sends.start(
+                    out.at[spots, cols], came_ref.at[k, spots, cols], token_sem.at[0, k, at],
+                    token_sem.at[1, k, at], near(k),
+                )
+            )
+
         out[:, :width] = plain(chosen, moe_ref[...]).astype(BF16)
-        out[:, width : 2 * width] = plain(chosen, cot_ref[...]).astype(BF16)
-        gate_out = gate_packed_ref.at[k - 1] if k else gate_came_ref.at[0]
-        gate_out[...] = as_row(jnp.sum(found * gates_row, axis=1, keepdims=True))
         if k == 2:
             pl.semaphore_wait(barrier, len(peers))
         if k:
-            token_copies[k] = []
-            cuts = [(0, capacity, 0)]
-            cuts += [(0, half, width), (half, half, width)] if k == 3 else [(0, capacity, width)]
-            for at, (begin, size, first) in enumerate(cuts):
-                spots, cols = pl.ds(begin, size), pl.ds(first, width)
-                if at == 1:
-                    gate_copies_in[k] = sends.start(
-                        gate_out, gate_came_ref.at[k], token_sem.at[0, k, 3], token_sem.at[1, k, 3], near(k)
-                    )
-                token_copies[k].append(
-                    sends.start(
-                        out.at[spots, cols], came_ref.at[k, spots, cols], token_sem.at[0, k, at],
-                        token_sem.at[1, k, at], near(k),
-                    )
-                )
+            send_tokens(0, capacity, 0)
+        gate_out[...] = as_row(jnp.sum(found * gates_row, axis=1, keepdims=True))
+        if k == 2:
+            loads[1].wait()
+            for load in loads[2:]:
+                load.start()
+        out[:, width : 2 * width] = plain(chosen, cot_ref[...]).astype(BF16)
+        if k:
+            gate_copies_in[k] = sends.start(
+                gate_out, gate_came_ref.at[k], token_sem.at[0, k, 3], token_sem.at[1, k, 3], near(k)
+            )
+            for begin, size in ((0, half), (half, capacity - half)) if k == 3 else ((0, capacity),):
+                send_tokens(begin, size, width)
     for k in range(1, groups):
         target_copies[k] = sends.start(
             targets_ref.at[0], targets_ref.at[k], target_sem.at[0, k], target_sem.at[1, k], near(k)
@@ -274,7 +280,7 @@
     hidden_2 = expert((2,), 1, 0, 1)
     project_near(1)
     hidden_3 = expert((3,), 1, capacity, 2, (0, half))
-    hidden_4 = expert((3,), 1, capacity, 2, (half, half), 1)
+    hidden_4 = expert((3,), 1, capacity, 2, (half, capacity - half), 1)
     hidden_t_ref[1] = jnp.concatenate([hidden_2, hidden_3, hidden_4], axis=0).T
     if not direct:
         rows_t_ref[1] = jnp.concatenate([came_ref[2, :, :width], came_ref[3, :, :width]], axis=0).T
@@ -319,8 +325,9 @@
     items = [item(j) for j in range(length - 1)] + [(place, None)]
     pair_copies = {}
 
-    def pair_sends():
-        for j, (home, _) in enumerate(items):
+    def pair_sends(first, stop):
+        for j in range(first, stop):
+            home = items[j][0]
             if not direct:
                 pair_up_out[j] = up_rows(2 * home + 1 - side, pl.ds(0, wide)).astype(BF16)
                 pair_copies[0, j] = sends.start(
@@ -382,30 +389,13 @@
                 if last or j < length - 1:
                     line_item(kind, j)
 
-    pair_sends()
-    for copy in other_copies:
-        copy.wait_recv()
-    ends((0, 0), (2, 0))
-    project_near(2)
-    ends((1, 0), (0, 1), (2, 1))
-    middles((0, 0), (2, 0))
-    project_far(0)
-    ends((1, 1))
-    middles((1, 0), (0, 1), (2, 1))
-    project_far(1)
-    middles((0, 2), (1, 1))
-    project_far(2)
-    middles((2, 2))
-
     base = (3 * blocks + block) * tokens
-    for at in (5, 6, 7):
-        loads[at].wait()
 
     def inverse_counts(start, shape):
         counts = base + start + 1 + lax.broadcasted_iota(jnp.int32, shape, 0)
         return 1.0 / counts.astype(F32)
 
-    for i in range(groups):
+    def ordered(i, first):
         if i:
             target_copies[i].wait_recv()
         targets = targets_ref[i, 0:1, :]
@@ -422,31 +412,64 @@
         for h in range(heads):
             cols = slice(h * head_dim, (h + 1) * head_dim)
             state = contract_rows(query_ref[at, cols], scaled[:, cols])
-            local_ref[h] = state + local_ref[h] if i else state
-
-    cuts = [(0, heads // 2), (heads // 2, heads - heads // 2)] if heads > 1 else [(0, heads)]
+            local_ref[h] = state if first else state + local_ref[h]
+
+    pair_sends(0, 1)
+    for copy in other_copies:
+        copy.wait_recv()
+    ends((0, 0), (2, 0))
+    pair_sends(1, length)
+    project_near(2)
+    ends((1, 0), (0, 1), (2, 1))
+    middles((0, 0), (2, 0))
+    project_far(0)
+    ends((1, 1))
+    middles((1, 0), (0, 1), (2, 1))
+    project_far(1)
+    middles((0, 2), (1, 1))
+    for at in (5, 6, 7):
+        loads[at].wait()
+    ordered(2, True)
+    ordered(3, False)
+    project_far(2)
+    ordered(0, False)
+    ordered(1, False)
+
+    some = heads // 2
 
     def state_copy(turn, at, device):
-        part = pl.ds(*cuts[at])
         return pltpu.make_async_remote_copy(
-            src_ref=state_out_ref.at[turn, part], dst_ref=state_in_ref.at[turn, part],
+            src_ref=state_out_ref.at[turn % 3, at], dst_ref=state_in_ref.at[turn, at],
             send_sem=state_sem.at[0, turn, at], recv_sem=state_sem.at[1, turn, at],
             device_id=device, device_id_type=MESH,
         )
 
     line_ref[...] = jnp.zeros_like(line_ref)
-
-    def send_state(chosen, at):
-        @pl.when(chosen * has_left == 1)
+    mine, theirs = side * some, (1 - side) * some
+    for at in range(some):
+        state_out_ref[0, at] = local_ref[theirs + at].astype(BF16)
+        state_copy(0, at, partner).start()
+
+    before_last = at_least(place, length - 2, 2 * length) * has_right
+    left_block = lax.rem(block + blocks - 2, blocks)
+
+    @pl.when((1 - has_right) * has_left == 1)
+    def _():
+        for at in range(some):
+            state_out_ref[1, at] = local_ref[mine + at].astype(BF16)
+            state_copy(1, at, {"ctx": left_block}).start()
+            state_copy(3, at, {"ctx": lax.rem(left_block + 1 - 2 * side + blocks, blocks)}).start()
+
+    def send_state(at):
+        @pl.when(has_right * has_left == 1)
         def _():
-            part = pl.ds(*cuts[at])
-            state_out_ref[0, part] = (local_ref[part] + line_ref[part]).astype(BF16)
-            state_copy(0, at, {"ctx": lax.rem(block + blocks - 2, blocks)}).start()
-
-    for at in range(len(cuts)):
-        send_state(1 - has_right, at)
+            total = local_ref[mine + at] + state_in_ref[0, at].astype(F32)
+            state_out_ref[1, at] = (total + line_ref[at]).astype(BF16)
+            state_copy(1, at, {"ctx": left_block}).start()
+
     for j in range(2, length - 1):
         ends((0, j), (2, j), (1, j))
+    middles((2, 2))
 
     own = jnp.concatenate([placing(flipped(me, j), own_target).astype(BF16) for j in range(groups)], axis=0)
     rows = jnp.concatenate([rows_ref[j, j * capacity : (j + 1) * capacity, :] for j in range(groups)], axis=0)
@@ -476,7 +499,7 @@
 
     def backward(h, carry):
         cols = pl.ds(pl.multiple_of(h * head_dim, head_dim), head_dim)
-        state = line_ref[h]
+        state = later_ref[h]
         for at in reversed(range(tokens // chunk)):
             rows = pl.ds(at * chunk, chunk)
             query, keys = query_ref[rows, cols], key_ref[rows, cols]
@@ -491,45 +514,62 @@
 
     loads[8].wait()
     lax.fori_loop(0, heads, forward, 0)
-    for at, cut in enumerate(cuts):
-        part = pl.ds(*cut)
+    sends.drain()
+    finals = [(0, length - 1), (2, length - 1), (1, length - 1)]
+    ends(*finals, last=True)
+    for at in range(some):
+        state_copy(0, at, partner).wait_recv()
 
         @pl.when(has_right == 1)
         def _():
-            state_copy(0, at, partner).wait_recv()
-            line_ref[part] = state_in_ref[0, part].astype(F32)
-
-        send_state(has_right, at)
-        state_out_ref[1, part] = (line_ref[part] + local_ref[part] * side.astype(F32)).astype(BF16)
-        state_copy(1, at, partner).start()
+            state_copy(1, at, partner).wait_recv()
+            line_ref[at] = state_in_ref[1, at].astype(F32)
+
+        @pl.when(before_last == 1)
+        def _():
+            state_copy(3, at, partner).wait_recv()
+            line_ref[at] += state_in_ref[3, at].astype(F32)
+
+        send_state(at)
+        state_out_ref[2, at] = (line_ref[at] + local_ref[mine + at] * side.astype(F32)).astype(BF16)
+        state_copy(2, at, partner).start()
+        later_ref[mine + at] = line_ref[at] + state_in_ref[0, at].astype(F32) * (1 - side).astype(F32)
     middles((1, 2))
     for j in range(3, length - 1):
         middles((0, j), (2, j), (1, j))
-    finals = [(0, length - 1), (2, length - 1), (1, length - 1)]
-    ends(*finals, last=True)
-    for at, (begin, size) in enumerate(cuts):
-        part = pl.ds(begin, size)
-        state_copy(1, at, partner).wait_recv()
-        line_ref[part] += state_in_ref[1, part].astype(F32)
-        lax.fori_loop(begin, begin + size, backward, 0)
+    lax.fori_loop(mine, mine + some, backward, 0)
+    for at in range(some):
+        state_copy(2, at, partner).wait_recv()
+        later_ref[theirs + at] = state_in_ref[2, at].astype(F32)
+    lax.fori_loop(theirs, theirs + some, backward, 0)
     middles(*finals, last=True)
     for kind in range(3):
         for j in range(length - 1):
             line_copy(kind, j, 0, partner).wait_send()
 
-    for at in range(len(cuts)):
+    for at in range(some):
 
         @pl.when(has_left == 1)
         def _():
-            state_copy(0, at, partner).wait_send()
-
-        state_copy(1, at, partner).wait_send()
+            state_copy(1, at, partner).wait_send()
+
+        @pl.when((1 - has_right) * has_left == 1)
+        def _():
+            state_copy(3, at, partner).wait_send()
+
+        state_copy(0, at, partner).wait_send()
+        state_copy(2, at, partner).wait_send()
     sends.drain()
 
 
 def pass_kernel(count, *refs):
-    sems = refs[2 * count]
-    copies = [pltpu.make_async_copy(refs[at], refs[count + at], sems.at[at]) for at in range(count)]
+    sems, copies = refs[2 * count], []
+    for at in range(count):
+        rows = refs[at].shape[0]
+        cuts = 2 if rows % 32 == 0 else 1
+        for cut in range(cuts):
+            part = pl.ds(cut * (rows // cuts), rows // cuts)
+            copies.append(pltpu.make_async_copy(refs[at].at[part], refs[count + at].at[part], sems.at[at, cut]))
     for copy in copies:
         copy.start()
     for copy in copies:
@@ -542,7 +582,7 @@
         in_specs=[pl.BlockSpec(memory_space=pltpu.VMEM)] * len(arrays),
         out_specs=[pl.BlockSpec(memory_space=pl.ANY)] * len(arrays),
         out_shape=[jax.ShapeDtypeStruct(one.shape, one.dtype) for one in arrays],
-        scratch_shapes=[pltpu.SemaphoreType.DMA((len(arrays),))],
+        scratch_shapes=[pltpu.SemaphoreType.DMA((len(arrays), 2))],
         compiler_params=pltpu.CompilerParams(vmem_limit_bytes=1 << 20),
         name="pass_on",
     )(*[pltpu.with_memory_space_constraint(one, pltpu.VMEM) for one in arrays])
@@ -560,7 +600,6 @@
     tokens, cols = attn_query.shape
     heads, head_dim = prefix_state.shape[1:3]
     length = blocks // 2
-    turns = 2
     direct = unit % LANES == 0
     whole = pl.BlockSpec(memory_space=pltpu.VMEM)
     away = pl.BlockSpec(memory_space=pl.ANY)
@@ -581,9 +620,9 @@
         vmem((groups, groups * capacity, width), BF16), dma((2, groups, 3)),
         vmem((groups, groups * capacity, cols), BF16),
         flat_ref, flat_ref,
-        state, state,
-        vmem((turns, heads, head_dim, head_dim), BF16), vmem((turns, heads, head_dim, head_dim), BF16),
-        dma((2, turns, 2)),
+        state, vmem((heads // 2, head_dim, head_dim), F32), state,
+        vmem((3, heads // 2, head_dim, head_dim), BF16), vmem((4, heads // 2, head_dim, head_dim), BF16),
+        dma((2, 4, heads // 2)),
         vmem((length, unit_down, width), BF16), vmem((length, unit_down, width), BF16), dma((2, 2, length)),
         vmem((length - 1, unit, wide), BF16), vmem((length + 1, unit, wide), BF16),
         vmem((length - 1, unit_down, width), BF16), vmem((length + 1, unit_down, width), BF16),

time: 106 us -> 105 us (level)
  no operation moved by 1% of the time
where the time goes in v4:
time: 105 us; the launch traced here: 104 us
  Pallas kernels  103 us (98%)
    pallas_call x1, Pallas kernels, compute(): pl.pallas_call(functools.partial(layer_kernel, groups, blocks, min(256, t...  101 us
    pallas_call x1, Pallas kernels, pass_on(): pl.pallas_call(functools.partial(pass_kernel, len(arrays)), in_specs=[pl....  2.61 us

profile of v4, /device:TPU:16, one launch (start us, length us, event | category | flops | bytes accessed | tf_op | source)
XLA Modules:
  0.0 104.1 jit_solution(14113637510031568696)
XLA Ops:
  0.6 100.7 %layer.1 = (bf16[1024,512]{1,0:T(8,128)(2,1)S(1)}, bf16[1024,512]{1,0:T(8,128)(2,1)S(1)}, bf16[1024,512]{1,0:T(8,128)(2,1)S(1)}, bf16[256,2048]{1,0:T(8,128)(2,1...) custom-call(s32[1,256]{1,0:T(1,128)} %bitcast.11, bf16[1,256]{1,0:T(2,128)(2,1)} %bitcast.12, ...), custom_call_target="tpu_custom_call" | custom-call | tf_op jit(solution)/shard_map/layer/pallas_call | solution.py:641
  101.3 2.6 %pass_on.1 = (bf16[1024,512]{1,0:T(8,128)(2,1)}, bf16[1024,512]{1,0:T(8,128)(2,1)}, bf16[1024,512]{1,0:T(8,128)(2,1)}, bf16[256,2048]{1,0:T(8,128)(2,1)}, bf16[1...) custom-call(bf16[1024,512]{1,0:T(8,128)(2,1)S(1)} %get-tuple-element.21.refs_0_, ...), custom_call_target="tpu_custom_call" | custom-call | tf_op jit(solution)/shard_map/pass_on/pallas_call | solution.py:580
